TPU v7x, 32 devices: a whole 2x2x4 slice. The times are simulated.
32 devices in a mesh: blk: 16 (over z, y, core), rep: 2 (over x).
Axes of the slice: x: 2, y: 2, z: 4, core: 2. Of those that a mesh axis runs over, the one named last changes fastest.
Arguments:
- raw_integrals: float32 [16, 1024, 512], P(None, 'blk'), may hold values from -0.6 to 0.6
- virtual_coeffs: float32 [512, 256], P(None, 'rep'), may hold values from -0.25 to 0.25
- metric_root: float32 [1024, 1024], P(None, 'rep'), may hold values from -1 to 3, as said below
- occ_energies: float32 [16], P('blk'), may hold values from -2 to -0.5
- virt_energies: float32 [256], replicated, may hold values from 0.2 to 3
Outputs:
- gamma: float32 [16, 256, 1024], P('blk', None, 'rep')
Inputs may be any that keep to these rules, and one draw needn't show every extreme that they name: metric_root is exactly symmetric.
All inputs are finite; a program needn't handle non-finite values.
Results may differ from a plain program's by a relative error of at most 0.0001.
Values sent between devices are 32-bit elements; how exact they have to be, the bound alone decides.
No kernel may reach another device: no remote copies, remote signals or barrier semaphores. Data moves between devices by JAX's collectives and lax.ppermute only.
A program may use at most 64 MiB of HBM per device.

v0:
```python
import jax
import jax.numpy as jnp
from jax import lax
from jax.sharding import PartitionSpec as P

TURNS = 2


def from_behind(x, axis, by):
    count = lax.axis_size(axis)
    return lax.ppermute(x, axis, [(i, (i + by) % count) for i in range(count)])


def pair_terms(own_rows, own_eps, other_rows, other_eps, virt_energies, gradient):
    highest = lax.Precision.HIGHEST
    coulomb = jnp.einsum("xaq,ybq->xyab", own_rows, other_rows, precision=highest)
    spread = virt_energies[:, None] + virt_energies[None, :]
    denominator = spread[None, None] - own_eps[:, None, None, None] - other_eps[None, :, None, None]
    amplitude = (2.0 * coulomb - jnp.swapaxes(coulomb, 2, 3)) / denominator
    return gradient + jnp.einsum("xyab,ybq->xaq", amplitude, other_rows, precision=highest)


def per_device(raw_integrals, virtual_coeffs, metric_root, occ_energies, virt_energies):
    highest = lax.Precision.HIGHEST
    halfway = jnp.einsum("ipm,ma->ipa", raw_integrals, virtual_coeffs, precision=highest)
    regrouped = lax.all_to_all(halfway, "blk", split_axis=0, concat_axis=1, tiled=True)
    complete = lax.all_gather(regrouped, "rep", axis=2, tiled=True)
    fitted_part = jnp.einsum("xpa,pq->xaq", complete, metric_root, precision=highest)
    fitted = lax.all_gather(fitted_part, "rep", axis=2, tiled=True)
    replica = lax.axis_index("rep")
    replicas = lax.axis_size("rep")
    turns = TURNS
    turn_unit = 1
    travel_rows = fitted
    travel_eps = occ_energies
    for bit_index in range((replicas - 1).bit_length()):
        shifted_rows, shifted_eps = from_behind(
            (travel_rows, travel_eps), "blk", (1 << bit_index) * turns
        )
        chosen = replica >> bit_index & 1 == 1
        travel_rows = jnp.where(chosen, shifted_rows, travel_rows)
        travel_eps = jnp.where(chosen, shifted_eps, travel_eps)
    gradient = jnp.zeros(fitted.shape, jnp.float32)

    def advance(turn_index, state_now):
        other_rows, other_eps, total = state_now
        total = pair_terms(fitted, occ_energies, other_rows, other_eps, virt_energies, total)
        other_rows, other_eps = from_behind((other_rows, other_eps), "blk", turn_unit)
        return (other_rows, other_eps, total)

    travel_rows, travel_eps, gradient = lax.fori_loop(
        0, turns - 1, advance, (travel_rows, travel_eps, gradient)
    )
    gradient = pair_terms(fitted, occ_energies, travel_rows, travel_eps, virt_energies, gradient)
    return lax.psum_scatter(gradient, "rep", scatter_dimension=2, tiled=True)


def solution(mesh):
    return jax.shard_map(
        per_device,
        mesh=mesh,
        in_specs=(P(None, "blk", None), P(None, "rep"), P(None, "rep"), P("blk"), P()),
        out_specs=P("blk", None, "rep"),
        check_vma=False,
    )
```

profile of v0, /device:TPU:0, one launch (start us, length us, event | category | flops | bytes accessed | tf_op | source)
XLA Modules:
  0.0 165.9 jit_solution(520824804438171857)
XLA Ops:
  6.5 0.0 copy-start
  6.5 0.0 all-gather.4.cloned.1.call-start
  6.5 1.6 copy-done
  8.1 2.7 %fusion.18 = f32[16,64,128]{2,1,0:T(8,128)S(1)} fusion(f32[16,64,512]{2,1,0:T(8,128)S(1)} %copy-done, f32[512,128]{1,0:T(8,128)} %param.6), kind=kOutput, calls=%fused_computation.20 | convolution fusion | flops 805306368 | bytes 2883584 | tf_op jit(solution)/shard_map/ipm,ma->ipa/dot_general | solution.py:25
  10.9 21.6 %all_to_all.12 = f32[16,64,128]{2,1,0:T(8,128)} all-to-all(f32[16,64,128]{2,1,0:T(8,128)S(1)} %fusion.18), channel_id=1, replica_groups=mesh['blk'=16,'rep'=2] {'blk'}, dimensions={0} | all-to-all | bytes 1048576 | tf_op jit(solution)/shard_map/all_to_all | solution.py:26
  32.5 0.0 all-gather.4.cloned.1.call-update
  32.5 0.0 all-gather.6.cloned.1.call-start
  32.5 20.9 %all-gather.4.cloned.1.call-done = f32[1,1024,256]{2,1,0:T(8,128)} async-done(((f32[1,1024,128]{2,1,0:T(8,128)}), f32[1,1024,256]{2,1,0:T(8,128)}) %all-gather.4.cloned.1.call-update) | async-done | bytes 1048592 | tf_op jit(solution)/shard_map/all_gather | solution.py:27
  53.4 4.6 %fusion.8 = f32[256,512]{1,0:T(8,128)} fusion(f32[1024,512]{1,0:T(8,128)} %param.7, f32[1,1024,256]{2,1,0:T(8,128)} %all-gather.4.cloned.1.call-done), kind=kOutput, calls=%fused_computation.9 | convolution fusion | flops 1610612736 | bytes 3670016 | tf_op jit(solution)/shard_map/xpa,pq->xaq/dot_general | solution.py:28
  58.0 0.0 all-gather.6.cloned.1.call-update
  58.1 0.0 reduce-scatter.2.cloned.1.call-start
  58.1 21.4 %all-gather.6.cloned.1.call-done = f32[256,1024]{1,0:T(8,128)} async-done(((f32[256,512]{1,0:T(8,128)}), f32[256,1024]{1,0:T(8,128)}) %all-gather.6.cloned.1.call-update) | async-done | bytes 1048592 | tf_op jit(solution)/shard_map/all_gather | solution.py:29
  79.5 1.5 collective-permute-start
  81.0 26.3 %collective-permute-done = f32[1,256,1024]{2,1,0:T(8,128)} collective-permute-done((f32[1,256,1024]{2,1,0:T(8,128)}, f32[1,256,1024]{2,1,0:T(8,128)}, u32[]{:S(2)}, u32[]{:S(2)}) %collective-permute-start) | collective-permute-done | bytes 1048608 | tf_op jit(solution)/shard_map/ppermute | solution.py:11
  107.3 2.4 %broadcast_select_fusion = f32[1,256,1024]{2,1,0:T(8,128)} fusion(f32[1,256,1024]{2,1,0:T(8,128)} %collective-permute-done, pred[]{:T(512)} %eq.3, f32[256,1024]{1,0:T(8,128)} %all-gather.6.cloned.1.call-done), kind=kLoop, calls=%fused_computation.11 | loop fusion | flops 262144 | bytes 3145729 | tf_op jit(solution)/shard_map/jit(_where)/select_n | solution.py:41
  109.7 0.0 collective-permute-start.2
  109.7 0.0 collective-permute-start.1
  110.3 5.7 %collective-permute-done.1 = f32[1]{0:T(128)} collective-permute-done((f32[1]{0:T(128)}, f32[1]{0:T(128)}, u32[]{:S(2)}, u32[]{:S(2)}) %collective-permute-start.1) | collective-permute-done | bytes 36 | tf_op jit(solution)/shard_map/ppermute | solution.py:11
  116.7 11.9 %collective-permute-start.3 = (f32[1]{0:T(128)}, f32[1]{0:T(128)}, u32[]{:S(2)}, u32[]{:S(2)}) collective-permute-start(f32[1]{0:T(128)} %select_n.19), channel_id=1, source_target_pairs={{0,2},{2,4},{4,6},{6,8},{8,10},{10,12},{12,14},{14,16},{16,18},{18... | collective-permute-start | bytes 20 | tf_op jit(solution)/shard_map/while/body/eval_jaxpr/ppermute | solution.py:11
  128.6 0.0 copy-done.1
  128.6 2.3 %fusion.6 = f32[256,256]{1,0:T(8,128)S(1)} fusion(f32[256,1024]{1,0:T(8,128)S(1)} %copy-done.1, f32[1,256,1024]{2,1,0:T(8,128)} %broadcast_select_fusion), kind=kOutput, calls=%fused_computation.7 | convolution fusion | flops 805306368 | bytes 2359296 | tf_op jit(solution)/shard_map/while/body/eval_jaxpr/xaq,ybq->xyab/dot_general | solution.py:16
  130.8 0.0 copy-start.3
  130.9 0.9 copy.6
  131.7 0.0 collective-permute-done.2
  131.7 3.0 %fusion.3 = f32[256,256]{1,0:T(8,128)} fusion(f32[256,1024]{1,0:T(8,128)S(1)} %copy-done.1, f32[1,256,1024]{2,1,0:T(8,128)} %collective-permute-done.2), kind=kOutput, calls=%fused_computation.4 | convolution fusion | flops 805306368 | bytes 2359296 | tf_op jit(solution)/shard_map/xaq,ybq->xyab/dot_general | solution.py:16
  134.7 1.1 copy.8
  135.8 0.0 copy-done.3
  135.8 3.1 %fusion.1 = f32[256,1024]{1,0:T(8,128)S(1)} fusion(f32[1,256,1024]{2,1,0:T(8,128)} %collective-permute-done.2, f32[256,256]{1,0:T(8,128)} %fusion.3, f32[256,256]{0,1:T(8,128)S(1)} %copy.8, f32[]{:T(128)} %bitcast.17, f32[]{:T(128)} %bitcast.66, f32[256]{0:T(256)S(1)} %copy-done.3), kind=kOutput, calls=%fused_computation.2 | convolution fusion | flops 805699584 | bytes 2622472 | tf_op jit(solution)/shard_map/xyab,ybq->xaq/dot_general | solution.py:20
  138.9 0.0 copy-done.2
  138.9 3.3 %fusion = f32[1,256,1024]{2,1,0:T(8,128)} fusion(f32[256,1024]{1,0:T(8,128)S(1)} %fusion.1, f32[1,256,1024]{2,1,0:T(8,128)} %broadcast_select_fusion, f32[256,256]{1,0:T(8,128)S(1)} %fusion.6, f32[256,256]{0,1:T(8,128)S(1)} %copy-done.2, f32[]{:T(128)} %bitcast.11, f32[]{:T(128)} %bitcast.65, f32[256]{0:T(256)S(1)} %copy-done.3), kind=kOutput, calls=%fused_computation.1 | convolution fusion | flops 805961728 | bytes 3671048 | tf_op jit(solution)/shard_map/while/body/eval_jaxpr/xyab,ybq->xaq/dot_general | solution.py:20
  142.2 0.0 reduce-scatter.2.cloned.1.call-update
  142.3 17.1 %reduce-scatter.2.cloned.1.call-done = f32[1,256,512]{2,1,0:T(8,128)} async-done(((f32[1,256,1024]{2,1,0:T(8,128)}), f32[1,256,512]{2,1,0:T(8,128)}) %reduce-scatter.2.cloned.1.call-update) | async-done | bytes 524304 | tf_op jit(solution)/shard_map/reduce_scatter | solution.py:55
  (3 shorter events, 0.0 us)
Async XLA Ops:
  6.5 1.6 copy-start
  6.5 46.9 %all-gather.4.cloned.1.call-start = ((), (), s32[]{:S(2)}) async-start(), calls=%async_computation.2 | async-start | bytes 1572864 | tf_op jit(solution)/shard_map/all_gather | solution.py:27
  32.5 47.0 %all-gather.6.cloned.1.call-start = ((), (), s32[]{:S(2)}) async-start(), calls=%async_computation.4 | async-start | bytes 1572864 | tf_op jit(solution)/shard_map/all_gather | solution.py:29
  58.1 101.3 %reduce-scatter.2.cloned.1.call-start = ((), (), s32[]{:S(2)}) async-start(), calls=%async_computation.3 | async-start | bytes 1572864 | tf_op jit(solution)/shard_map/reduce_scatter | solution.py:55
  79.5 49.1 %copy-start.1 = (f32[256,1024]{1,0:T(8,128)S(1)}, f32[256,1024]{1,0:T(8,128)}, u32[]{:S(2)}) copy-start(f32[256,1024]{1,0:T(8,128)} %all-gather.6.cloned.1.call-done) | copy-start | bytes 3145732
  79.5 27.7 %collective-permute-start = (f32[1,256,1024]{2,1,0:T(8,128)}, f32[1,256,1024]{2,1,0:T(8,128)}, u32[]{:S(2)}, u32[]{:S(2)}) collective-permute-start(f32[1,256,1024]{2,1,0:T(8,128)} %bitcast.67), channel_id=1, source_target_pairs={{0,4},{2,6},{4,8},{6,10},{8,12},{10,14},{12,16},{14,18},{16,20},{1... | collective-permute-start | bytes 3145736 | tf_op jit(solution)/shard_map/ppermute | solution.py:11
  109.7 22.1 %collective-permute-start.2 = (f32[1,256,1024]{2,1,0:T(8,128)}, f32[1,256,1024]{2,1,0:T(8,128)}, u32[]{:S(2)}, u32[]{:S(2)}) collective-permute-start(f32[1,256,1024]{2,1,0:T(8,128)} %broadcast_select_fusion), channel_id=1, source_target_pairs={{0,2},{2,4},{4,6},{6,8},{8,10},{10,12},{12,14},{14,16},{16,18},{18... | collective-permute-start | bytes 3145736 | tf_op jit(solution)/shard_map/while/body/eval_jaxpr/ppermute | solution.py:11
  109.7 6.4 %collective-permute-start.1 = (f32[1]{0:T(128)}, f32[1]{0:T(128)}, u32[]{:S(2)}, u32[]{:S(2)}) collective-permute-start(f32[1]{0:T(128)} %param.8), channel_id=1, source_target_pairs={{0,4},{2,6},{4,8},{6,10},{8,12},{10,14},{12,16},{14,18},{16,20},{1... | collective-permute-start | bytes 20 | tf_op jit(solution)/shard_map/ppermute | solution.py:11
  116.7 19.1 %collective-permute-start.3 = (f32[1]{0:T(128)}, f32[1]{0:T(128)}, u32[]{:S(2)}, u32[]{:S(2)}) collective-permute-start(f32[1]{0:T(128)} %select_n.19), channel_id=1, source_target_pairs={{0,2},{2,4},{4,6},{6,8},{8,10},{10,12},{12,14},{14,16},{16,18},{18... | collective-permute-start | bytes 20 | tf_op jit(solution)/shard_map/while/body/eval_jaxpr/ppermute | solution.py:11
  130.8 5.0 %copy-start.3 = (f32[256]{0:T(256)S(1)}, f32[256]{0:T(256)}, u32[]{:S(2)}) copy-start(f32[256]{0:T(256)} %param.9) | copy-start | bytes 3076
  134.7 4.2 %copy-start.2 = (f32[256,256]{0,1:T(8,128)S(1)}, f32[256,256]{0,1:T(8,128)}, u32[]{:S(2)}) copy-start(f32[256,256]{0,1:T(8,128)} %copy.6) | copy-start | bytes 786436
Sparse Core Ops, SparseCore 0:
  32.6 20.7 all-gather.3
  58.2 21.2 all-gather.5
  142.4 16.9 reduce-scatter.1
where the time goes:
time: 166 us
  waiting for transfers between devices  91.4 us (55%)
  blocking collectives  21.6 us (13%)
  matrix products  19 us (11%)
  between operations  14.6 us (9%)
  starting transfers between devices  13.4 us (8%)
  local copies, waits for them, and re-layouts  3.58 us (2%)
  other arithmetic  2.4 us (1%)
    ppermute x4, waiting for transfers between devices, from_behind(): return lax.ppermute(x, axis, [(i, (i + by) % count) for i in range(count)])  31.9 us
    all_to_all x1, blocking collectives, per_device(): lax.all_to_all(halfway, 'blk', split_axis=0, concat_axis=1, tiled=True)  21.6 us
    all_gather x1, waiting for transfers between devices, per_device(): fitted = lax.all_gather(fitted_part, 'rep', axis=2, tiled=True)  21.4 us
    all_gather x1, waiting for transfers between devices, per_device(): complete = lax.all_gather(regrouped, 'rep', axis=2, tiled=True)  20.9 us
    reduce_scatter x1, waiting for transfers between devices, per_device(): return lax.psum_scatter(gradient, 'rep', scatter_dimension=2, tiled=True)  17.1 us
    ppermute x4, starting transfers between devices, from_behind(): return lax.ppermute(x, axis, [(i, (i + by) % count) for i in range(count)])  13.3 us
    dot_general x2, matrix products, pair_terms(): jnp.einsum('xyab,ybq->xaq', amplitude, other_rows, precision=highest)  6.38 us
    dot_general x2, matrix products, pair_terms(): jnp.einsum('xaq,ybq->xyab', own_rows, other_rows, precision=highest)  5.22 us
  transfers between devices with their start and end apart: 7, of which 5 were waited for; matrix products, arithmetic and copies ran while one was open for 4% of the time, Pallas kernels for 0%

commit v1 on v0

--- a/solution.py
+++ b/solution.py
@@ -20,7 +20,7 @@
     return gradient + jnp.einsum("xyab,ybq->xaq", amplitude, other_rows, precision=highest)
 
 
-def per_device(raw_integrals, virtual_coeffs, metric_root, occ_energies, virt_energies):
+def any_replicas(raw_integrals, virtual_coeffs, metric_root, occ_energies, virt_energies):
     highest = lax.Precision.HIGHEST
     halfway = jnp.einsum("ipm,ma->ipa", raw_integrals, virtual_coeffs, precision=highest)
     regrouped = lax.all_to_all(halfway, "blk", split_axis=0, concat_axis=1, tiled=True)
@@ -29,13 +29,11 @@
     fitted = lax.all_gather(fitted_part, "rep", axis=2, tiled=True)
     replica = lax.axis_index("rep")
     replicas = lax.axis_size("rep")
-    turns = TURNS
-    turn_unit = 1
     travel_rows = fitted
     travel_eps = occ_energies
     for bit_index in range((replicas - 1).bit_length()):
         shifted_rows, shifted_eps = from_behind(
-            (travel_rows, travel_eps), "blk", (1 << bit_index) * turns
+            (travel_rows, travel_eps), "blk", (1 << bit_index) * TURNS
         )
         chosen = replica >> bit_index & 1 == 1
         travel_rows = jnp.where(chosen, shifted_rows, travel_rows)
@@ -45,14 +43,91 @@
     def advance(turn_index, state_now):
         other_rows, other_eps, total = state_now
         total = pair_terms(fitted, occ_energies, other_rows, other_eps, virt_energies, total)
-        other_rows, other_eps = from_behind((other_rows, other_eps), "blk", turn_unit)
+        other_rows, other_eps = from_behind((other_rows, other_eps), "blk", 1)
         return (other_rows, other_eps, total)
 
     travel_rows, travel_eps, gradient = lax.fori_loop(
-        0, turns - 1, advance, (travel_rows, travel_eps, gradient)
+        0, TURNS - 1, advance, (travel_rows, travel_eps, gradient)
     )
     gradient = pair_terms(fitted, occ_energies, travel_rows, travel_eps, virt_energies, gradient)
     return lax.psum_scatter(gradient, "rep", scatter_dimension=2, tiled=True)
+
+
+def dot(x, y, over_x, over_y):
+    return lax.dot_general(
+        x, y, (((over_x,), (over_y,)), ((), ())), precision=lax.Precision.HIGH
+    )
+
+
+def half_of(x, index, axis):
+    size = x.shape[axis] // 2
+    return lax.dynamic_slice_in_dim(x, index * size, size, axis)
+
+
+def two_replicas(raw_integrals, virtual_coeffs, metric_root, occ_energies, virt_energies):
+    blocks = lax.axis_size("blk")
+    block = lax.axis_index("blk")
+    rep = lax.axis_index("rep")
+    core = block % 2
+    swap = [(0, 1), (1, 0)]
+    mate = [(i, i ^ 1) for i in range(blocks)]
+    mine = half_of(metric_root, rep, 0)
+    across = half_of(metric_root, 1 - rep, 0)
+    there = lax.ppermute(half_of(mine, core, 0), "rep", swap)
+
+    halfway = jnp.einsum(
+        "ipm,ma->ipa", raw_integrals, virtual_coeffs, precision=lax.Precision.HIGH
+    )
+    note = jnp.broadcast_to(occ_energies[:, None, None], (halfway.shape[0], 8, halfway.shape[2]))
+    sent = jnp.concatenate([halfway, note], axis=1)
+    got = lax.all_to_all(sent, "blk", split_axis=0, concat_axis=0, tiled=True)
+    depth = halfway.shape[1]
+    rows = got[:, :depth].reshape(-1, got.shape[2])
+    all_eps = got[:, depth, 0]
+
+    there_mate = lax.ppermute(there, "blk", mate)
+    fit_mine = dot(rows, metric_root, 0, 0)
+    rows_there = half_of(rows, 1 - rep, 0)
+    fit_there = (
+        dot(half_of(rows, rep, 0), across, 0, 1)
+        + dot(half_of(rows_there, core, 0), there, 0, 0)
+        + dot(half_of(rows_there, 1 - core, 0), there_mate, 0, 0)
+    )
+    fit = jnp.where(
+        rep == 0,
+        jnp.concatenate([fit_mine, fit_there], 1),
+        jnp.concatenate([fit_there, fit_mine], 1),
+    )
+    fit_over = lax.ppermute(fit, "rep", swap)
+    behind = from_behind(fit, "blk", 2)
+    own = jnp.concatenate([fit, fit_over], 0)
+    behind_over = lax.ppermute(behind, "rep", swap)
+    far = lax.ppermute(own, "blk", [(i, (i + 1 + 2 * (i % 2)) % blocks) for i in range(blocks)])
+    near = jnp.concatenate([behind, behind_over], 0)
+    near_mate = lax.ppermute(near, "blk", mate)
+
+    eps = lambda index: lax.dynamic_index_in_dim(all_eps, index % blocks, 0, keepdims=False)
+    levels = jnp.where(rep == 0, virt_energies, jnp.roll(virt_energies, virt_energies.shape[0] // 2))
+    spread = levels[:, None] + levels[None, :] - eps(block)
+    total = 0.0
+    for other, index in (
+        (own, block),
+        (far, jnp.where(core == 0, block - 3, block - 1)),
+        (near, block - 2),
+        (near_mate, jnp.where(core == 0, block - 1, block - 3)),
+    ):
+        coulomb = dot(own, other, 1, 1)
+        amplitude = (2.0 * coulomb - coulomb.T) / (spread - eps(index))
+        total = total + dot(amplitude, half_of(other, rep, 1), 1, 0)
+    total = jnp.where(rep == 0, total, jnp.roll(total, total.shape[0] // 2, 0))
+    return total[None]
+
+
+def per_device(*arrays):
+    blocks = lax.axis_size("blk")
+    if lax.axis_size("rep") == 2 and TURNS == 2 and blocks % 2 == 0 and arrays[3].shape == (1,):
+        return two_replicas(*arrays)
+    return any_replicas(*arrays)
 
 
 def solution(mesh):

time: 166 us -> 89.3 us (0.54)
  waiting for transfers between devices: 91.4 us -> 36.5 us
  blocking collectives: 21.6 us -> 0 us
  between operations: 14.6 us -> 1 us
  local copies, waits for them, and re-layouts: 3.58 us -> 11.3 us
  matrix products: 19 us -> 25.2 us
    all_gather x2 -> x0, waiting for transfers between devices: 42.3 us -> none  [the longest x1 21.4 us: per_device(): fitted = lax.all_gather(fitted_part, 'rep', axis=2, tiled=True)]
    ppermute x0 -> x6, waiting for transfers between devices: none -> 33.5 us  [the longest x1 12.9 us: two_replicas(): there = lax.ppermute(half_of(mine, core, 0), 'rep', swap)]
    ppermute x4 -> x1, waiting for transfers between devices: 31.9 us -> 2.94 us  [from_behind(): return lax.ppermute(x, axis, [(i, (i + by) % count) for i in range(count)])]
    all_to_all x1 -> x0, blocking collectives: 21.6 us -> none  [per_device(): lax.all_to_all(halfway, 'blk', split_axis=0, concat_axis=1, tiled=True)]
    reduce_scatter x1 -> x0, waiting for transfers between devices: 17.1 us -> none  [per_device(): return lax.psum_scatter(gradient, 'rep', scatter_dimension=2, tiled=True)]
    ppermute x4 -> x1, starting transfers between devices: 13.3 us -> 1.63 us  [from_behind(): return lax.ppermute(x, axis, [(i, (i + by) % count) for i in range(count)])]
    all_to_all x0 -> x1, starting transfers between devices: none -> 7.41 us  [two_replicas(): got = lax.all_to_all(sent, 'blk', split_axis=0, concat_axis=0, tiled=True)]
    dot_general x6 -> x13, matrix products: 19 us -> 25.2 us  [the longest x12 22.6 us: dot(): lax.dot_general(x, y, (((over_x,), (over_y,)), ((), ())), precision=lax.P...]
  transfers between devices with their start and end apart: 7 -> 8, of which waited for: 5 -> 5; matrix products, arithmetic and copies ran while one was open for 4% -> 25% of each run, Pallas kernels for 0% -> 0%
where the time goes in v1:
time: 89.3 us; the launch traced here: 88.6 us
  waiting for transfers between devices  36.5 us (41%)
  matrix products  25.2 us (28%)
  starting transfers between devices  12.6 us (14%)
  local copies, waits for them, and re-layouts  11.3 us (13%)
  other arithmetic  1.99 us (2%)
  between operations  1 us (1%)
    dot_general x12, matrix products, dot(): lax.dot_general(x, y, (((over_x,), (over_y,)), ((), ())), precision=lax.P...  22.6 us
    ppermute x1, waiting for transfers between devices, two_replicas(): there = lax.ppermute(half_of(mine, core, 0), 'rep', swap)  12.9 us
    ppermute x1, waiting for transfers between devices, two_replicas(): fit_over = lax.ppermute(fit, 'rep', swap)  11.1 us
    ppermute x1, waiting for transfers between devices, two_replicas(): behind_over = lax.ppermute(behind, 'rep', swap)  9.36 us
    all_to_all x1, starting transfers between devices, two_replicas(): got = lax.all_to_all(sent, 'blk', split_axis=0, concat_axis=0, tiled=True)  7.41 us
    dot_general x4, local copies, waits for them, and re-layouts, dot(): lax.dot_general(x, y, (((over_x,), (over_y,)), ((), ())), precision=lax.P...  4.62 us
    ppermute x1, waiting for transfers between devices, from_behind(): return lax.ppermute(x, axis, [(i, (i + by) % count) for i in range(count)])  2.94 us
    unnamed x11, local copies, waits for them, and re-layouts  2.6 us
  transfers between devices with their start and end apart: 8, of which 5 were waited for; matrix products, arithmetic and copies ran while one was open for 25% of the time, Pallas kernels for 0%

profile of v1, /device:TPU:0, one launch (start us, length us, event | category | flops | bytes accessed | tf_op | source)
XLA Modules:
  0.0 88.6 jit_solution(17421297140919246725)
XLA Ops:
  0.8 2.6 %fusion.19 = f32[16,64,128]{2,1,0:T(8,128)S(1)} fusion(f32[16,64,512]{2,1,0:T(8,128)} %param.5, f32[512,128]{1,0:T(8,128)} %param.6), kind=kOutput, calls=%fused_computation.27 | convolution fusion | flops 402653184 | bytes 2883584 | tf_op jit(solution)/shard_map/ipm,ma->ipa/dot_general | solution.py:78
  3.4 0.9 concatenate.23
  4.3 7.4 %all-to-all-start = ((f32[16,72,128]{2,1,0:T(8,128)}), f32[16,72,128]{2,1,0:T(8,128)S(1)}, u32[]{:S(2)}, u32[]{:S(2)}) async-start(f32[16,72,128]{2,1,0:T(8,128)} %concatenate.23), calls=%async_computation | async-start | bytes 1179648 | tf_op jit(solution)/shard_map/all_to_all | solution.py:83
  11.7 0.9 constant_dynamic-slice_fusion.4
  12.6 1.5 %collective-permute-start = (f32[256,512]{1,0:T(8,128)}, f32[256,512]{1,0:T(8,128)S(1)}, u32[]{:S(2)}, u32[]{:S(2)}) collective-permute-start(f32[256,512]{1,0:T(8,128)} %constant_dynamic-slice_fusion.4), channel_id=1, source_target_pairs={{0,1},{1,0},{2,3},{3,2},{4,5},{5,4},{6,7},{7,6},{8,9},{9,8},{10,11... | collective-permute-start | bytes 1572872 | tf_op jit(solution)/shard_map/ppermute | solution.py:76
  14.1 12.9 %collective-permute-done = f32[256,512]{1,0:T(8,128)S(1)} collective-permute-done((f32[256,512]{1,0:T(8,128)}, f32[256,512]{1,0:T(8,128)S(1)}, u32[]{:S(2)}, u32[]{:S(2)}) %collective-permute-start) | collective-permute-done | bytes 524320 | tf_op jit(solution)/shard_map/ppermute | solution.py:76
  27.1 0.7 fusion.1
  28.2 0.7 fusion.69
  29.0 1.4 %convolution_add_fusion.2 = f32[128,512]{1,0:T(8,128)S(1)} fusion(f32[128,512]{1,0:T(8,128)S(1)} %convolution_add_fusion.3, f32[256,512]{1,0:T(8,128)} %collective-permute-done.1, f32[1024,128]{1,0:T(8,128)S(1)} %bitcast.43, s32[]{:T(128)S(6)} %dynamic_slice.58), kind=kOutput, calls=%fused_computation.6 | convolution fusion | flops 100728832 | bytes 1179652 | tf_op jit(solution)/shard_map/dot_general | solution.py:57
  30.5 1.6 %collective-permute-start.2 = (f32[128,1024]{1,0:T(8,128)S(1)}, f32[128,1024]{1,0:T(8,128)S(1)}, u32[]{:S(2)}, u32[]{:S(2)}) collective-permute-start(f32[128,1024]{1,0:T(8,128)S(1)} %maximum_select_fusion), channel_id=1, source_target_pairs={{0,1},{1,0},{2,3},{3,2},{4,5},{5,4},{6,7},{7,6},{8,9},{9,8},{10,11... | collective-permute-start | bytes 1572872 | tf_op jit(solution)/shard_map/ppermute | solution.py:101
  32.0 1.6 %collective-permute-start.4 = (f32[128,1024]{1,0:T(8,128)S(1)}, f32[128,1024]{1,0:T(8,128)}, u32[]{:S(2)}, u32[]{:S(2)}) collective-permute-start(f32[128,1024]{1,0:T(8,128)S(1)} %maximum_select_fusion), channel_id=1, source_target_pairs={{0,4},{2,6},{4,8},{6,10},{8,12},{10,14},{12,16},{14,18},{16,20},{1... | collective-permute-start | bytes 1572872 | tf_op jit(solution)/shard_map/ppermute | solution.py:11
  33.7 11.1 %collective-permute-done.2 = f32[128,1024]{1,0:T(8,128)S(1)} collective-permute-done((f32[128,1024]{1,0:T(8,128)S(1)}, f32[128,1024]{1,0:T(8,128)S(1)}, u32[]{:S(2)}, u32[]{:S(2)}) %collective-permute-start.2) | collective-permute-done | bytes 524320 | tf_op jit(solution)/shard_map/ppermute | solution.py:101
  44.7 1.1 %pad_maximum_fusion = f32[256,1024]{1,0:T(8,128)} fusion(f32[128,1024]{1,0:T(8,128)S(1)} %collective-permute-done.2, f32[128,1024]{1,0:T(8,128)S(1)} %maximum_select_fusion), kind=kLoop, calls=%fused_computation.1 | loop fusion | flops 262144 | bytes 2097152 | tf_op jit(solution)/shard_map/concatenate | solution.py:103
  45.8 2.9 %collective-permute-done.4 = f32[128,1024]{1,0:T(8,128)} collective-permute-done((f32[128,1024]{1,0:T(8,128)S(1)}, f32[128,1024]{1,0:T(8,128)}, u32[]{:S(2)}, u32[]{:S(2)}) %collective-permute-start.4) | collective-permute-done | bytes 524320 | tf_op jit(solution)/shard_map/ppermute | solution.py:11
  49.3 0.8 slice.29
  50.7 1.9 %constant_dynamic-update-slice_fusion.1 = f32[256,1024]{1,0:T(8,128)} fusion(f32[128,1024]{1,0:T(8,128)} %collective-permute-done.4), kind=kLoop, calls=%fused_computation.61 | loop fusion | bytes 1048576
  52.6 9.4 %collective-permute-done.5 = f32[128,1024]{1,0:T(8,128)S(1)} collective-permute-done((f32[128,1024]{1,0:T(8,128)}, f32[128,1024]{1,0:T(8,128)S(1)}, u32[]{:S(2)}, u32[]{:S(2)}) %collective-permute-start.5) | collective-permute-done | bytes 524320 | tf_op jit(solution)/shard_map/ppermute | solution.py:104
  62.0 0.8 constant_dynamic-update-slice_fusion
  62.8 0.6 fusion.66
  63.5 0.7 copy-done.1
  64.2 0.8 copy.6
  65.0 1.8 %fusion.63 = f32[256,256]{1,0:T(8,128)S(1)} fusion(f32[256,1024]{1,0:T(8,128)} %constant_dynamic-update-slice_fusion, f32[128,1024]{1,0:T(8,128)S(1)} %collective-permute-done.2, f32[128,1024]{1,0:T(8,128)S(1)} %maximum_select_fusion), kind=kOutput, calls=%fused_computation.80 | convolution fusion | flops 402915328 | bytes 2359296 | tf_op jit(solution)/shard_map/dot_general | solution.py:57
  66.9 0.8 copy.8
  67.7 2.5 %fusion.64 = f32[256,256]{1,0:T(8,128)} fusion(f32[256,1024]{1,0:T(8,128)} %collective-permute-done.3, f32[128,1024]{1,0:T(8,128)S(1)} %collective-permute-done.2, f32[128,1024]{1,0:T(8,128)S(1)} %maximum_select_fusion), kind=kOutput, calls=%fused_computation.81 | convolution fusion | flops 402915328 | bytes 2359296 | tf_op jit(solution)/shard_map/dot_general | solution.py:57
  70.3 1.8 %copy.7 = f32[256,256]{0,1:T(8,128)} copy(f32[256,256]{1,0:T(8,128)} %fusion.64) | data formatting | bytes 524288 | tf_op jit(solution)/shard_map/dot_general | solution.py:57
  72.1 3.0 %fusion.9 = f32[256,512]{1,0:T(8,128)S(1)} fusion(f32[256,1024]{1,0:T(8,128)} %collective-permute-done.3, s32[]{:T(128)S(6)} %select_n.98, f32[256,256]{1,0:T(8,128)} %fusion.64, f32[256,256]{0,1:T(8,128)} %copy.7, f32[]{:T(128)} %bitcast.6, f32[]{:T(128)} %bitcast.4, f32[256]{0:T(256)S(1)} %maximum_select_fusion.2), kind=kOutput, calls=%fused_computation.17 | convolution fusion | flops 201719808 | bytes 1575940 | tf_op jit(solution)/shard_map/dot_general | solution.py:57
  75.1 3.0 %convolution_add_fusion.1 = f32[256,512]{1,0:T(8,128)} fusion(f32[256,512]{1,0:T(8,128)S(1)} %fusion.9, s32[]{:T(128)S(6)} %select_n.98, f32[128,1024]{1,0:T(8,128)S(1)} %maximum_select_fusion, f32[128,1024]{1,0:T(8,128)S(1)} %collective-permute-done.2, f32[256,256]{1,0:T(8,128)} %copy-done.1, f32[256,256]{0,1:T(8,128)} %copy.6, f32[]{:T(128)} %bitcast.4, ...), kind=kOutput, calls=%fused_computation.5 | convolution fusion | flops 201981952 | bytes 2623496 | tf_op jit(solution)/shard_map/dot_general | solution.py:57
  78.1 2.5 %fusion.65 = f32[256,256]{1,0:T(8,128)} fusion(f32[256,1024]{1,0:T(8,128)} %collective-permute-done.6, f32[128,1024]{1,0:T(8,128)S(1)} %collective-permute-done.2, f32[128,1024]{1,0:T(8,128)S(1)} %maximum_select_fusion), kind=kOutput, calls=%fused_computation.82 | convolution fusion | flops 402915328 | bytes 2359296 | tf_op jit(solution)/shard_map/dot_general | solution.py:57
  80.7 1.1 %copy.9 = f32[256,256]{0,1:T(8,128)S(1)} copy(f32[256,256]{1,0:T(8,128)} %fusion.65) | data formatting | bytes 524288 | tf_op jit(solution)/shard_map/dot_general | solution.py:57
  81.8 2.9 %fusion.6 = f32[256,512]{1,0:T(8,128)S(1)} fusion(f32[256,1024]{1,0:T(8,128)} %collective-permute-done.6, s32[]{:T(128)S(6)} %select_n.98, f32[256,256]{1,0:T(8,128)} %fusion.65, f32[256,256]{0,1:T(8,128)S(1)} %copy.9, f32[]{:T(128)} %bitcast.10, f32[]{:T(128)} %bitcast.4, f32[256]{0:T(256)S(1)} %maximum_select_fusion.2), kind=kOutput, calls=%fused_computation.14 | convolution fusion | flops 201719808 | bytes 1575940 | tf_op jit(solution)/shard_map/dot_general | solution.py:57
  84.7 3.0 %fusion = f32[256,512]{1,0:T(8,128)S(1)} fusion(f32[256,512]{1,0:T(8,128)S(1)} %fusion.6, f32[256,512]{1,0:T(8,128)S(1)} %copy-done.3, f32[256,1024]{1,0:T(8,128)} %constant_dynamic-update-slice_fusion, s32[]{:T(128)S(6)} %select_n.98, f32[256,256]{1,0:T(8,128)S(1)} %fusion.63, f32[256,256]{0,1:T(8,128)} %copy.8, f32[]{:T(128)} %bitcast.8, f32[]{:T(128)} %bitcast.4, ...), kind=kOutput, calls=%fused_computation.4 | convolution fusion | flops 201981952 | bytes 2624516 | tf_op jit(solution)/shard_map/dot_general | solution.py:57
  87.7 0.9 fusion.5
  (24 shorter events, 1.8 us)
Async XLA Ops:
  0.0 11.7 %copy-start = (f32[1024,512]{1,0:T(8,128)S(1)}, f32[1024,512]{1,0:T(8,128)}, u32[]{:S(2)}) copy-start(f32[1024,512]{1,0:T(8,128)} %param.7) | copy-start | bytes 6291460
  4.3 22.8 %all-to-all-start = ((f32[16,72,128]{2,1,0:T(8,128)}), f32[16,72,128]{2,1,0:T(8,128)S(1)}, u32[]{:S(2)}, u32[]{:S(2)}) async-start(f32[16,72,128]{2,1,0:T(8,128)} %concatenate.23), calls=%async_computation | async-start | bytes 1179648 | tf_op jit(solution)/shard_map/all_to_all | solution.py:83
  12.6 14.4 %collective-permute-start = (f32[256,512]{1,0:T(8,128)}, f32[256,512]{1,0:T(8,128)S(1)}, u32[]{:S(2)}, u32[]{:S(2)}) collective-permute-start(f32[256,512]{1,0:T(8,128)} %constant_dynamic-slice_fusion.4), channel_id=1, source_target_pairs={{0,1},{1,0},{2,3},{3,2},{4,5},{5,4},{6,7},{7,6},{8,9},{9,8},{10,11... | collective-permute-start | bytes 1572872 | tf_op jit(solution)/shard_map/ppermute | solution.py:76
  27.0 2.0 %collective-permute-start.1 = (f32[256,512]{1,0:T(8,128)S(1)}, f32[256,512]{1,0:T(8,128)}, u32[]{:S(2)}, u32[]{:S(2)}) collective-permute-start(f32[256,512]{1,0:T(8,128)S(1)} %collective-permute-done), channel_id=1, source_target_pairs={{0,2},{2,0},{4,6},{6,4},{8,10},{10,8},{12,14},{14,12},{16,18},{18,... | collective-permute-start | bytes 1572872 | tf_op jit(solution)/shard_map/ppermute | solution.py:88
  27.1 1.9 %copy-start.2 = (f32[16,72,128]{2,1,0:T(8,128)}, f32[16,72,128]{2,1,0:T(8,128)S(1)}, u32[]{:S(2)}) copy-start(f32[16,72,128]{2,1,0:T(8,128)S(1)} %all-to-all-done) | copy-start | bytes 1769476
  28.9 20.4 %copy-start.4 = (f32[256]{0:T(256)S(1)}, f32[256]{0:T(256)}, u32[]{:S(2)}) copy-start(f32[256]{0:T(256)} %param.9) | copy-start | bytes 3076
  30.5 14.3 %collective-permute-start.2 = (f32[128,1024]{1,0:T(8,128)S(1)}, f32[128,1024]{1,0:T(8,128)S(1)}, u32[]{:S(2)}, u32[]{:S(2)}) collective-permute-start(f32[128,1024]{1,0:T(8,128)S(1)} %maximum_select_fusion), channel_id=1, source_target_pairs={{0,1},{1,0},{2,3},{3,2},{4,5},{5,4},{6,7},{7,6},{8,9},{9,8},{10,11... | collective-permute-start | bytes 1572872 | tf_op jit(solution)/shard_map/ppermute | solution.py:101
  32.0 16.7 %collective-permute-start.4 = (f32[128,1024]{1,0:T(8,128)S(1)}, f32[128,1024]{1,0:T(8,128)}, u32[]{:S(2)}, u32[]{:S(2)}) collective-permute-start(f32[128,1024]{1,0:T(8,128)S(1)} %maximum_select_fusion), channel_id=1, source_target_pairs={{0,4},{2,6},{4,8},{6,10},{8,12},{10,14},{12,16},{14,18},{16,20},{1... | collective-permute-start | bytes 1572872 | tf_op jit(solution)/shard_map/ppermute | solution.py:11
  45.8 21.9 %collective-permute-start.3 = (f32[256,1024]{1,0:T(8,128)}, f32[256,1024]{1,0:T(8,128)}, u32[]{:S(2)}, u32[]{:S(2)}) collective-permute-start(f32[256,1024]{1,0:T(8,128)} %pad_maximum_fusion), channel_id=1, source_target_pairs={{0,2},{2,8},{4,6},{6,12},{8,10},{10,16},{12,14},{14,20},{16,18},{1... | collective-permute-start | bytes 3145736 | tf_op jit(solution)/shard_map/ppermute | solution.py:105
  48.7 13.3 %collective-permute-start.5 = (f32[128,1024]{1,0:T(8,128)}, f32[128,1024]{1,0:T(8,128)S(1)}, u32[]{:S(2)}, u32[]{:S(2)}) collective-permute-start(f32[128,1024]{1,0:T(8,128)} %collective-permute-done.4), channel_id=1, source_target_pairs={{0,1},{1,0},{2,3},{3,2},{4,5},{5,4},{6,7},{7,6},{8,9},{9,8},{10,11... | collective-permute-start | bytes 1572872 | tf_op jit(solution)/shard_map/ppermute | solution.py:104
  62.8 15.3 %collective-permute-start.6 = (f32[256,1024]{1,0:T(8,128)}, f32[256,1024]{1,0:T(8,128)}, u32[]{:S(2)}, u32[]{:S(2)}) collective-permute-start(f32[256,1024]{1,0:T(8,128)} %constant_dynamic-update-slice_fusion), channel_id=1, source_target_pairs={{0,2},{2,0},{4,6},{6,4},{8,10},{10,8},{12,14},{14,12},{16,18},{18,... | collective-permute-start | bytes 3145736 | tf_op jit(solution)/shard_map/ppermute | solution.py:107
  63.5 0.7 copy-start.1
  80.7 4.0 %copy-start.3 = (f32[256,512]{1,0:T(8,128)S(1)}, f32[256,512]{1,0:T(8,128)}, u32[]{:S(2)}) copy-start(f32[256,512]{1,0:T(8,128)} %convolution_add_fusion.1) | copy-start | bytes 1572868

commit v2 on v0

--- a/solution.py
+++ b/solution.py
@@ -1,9 +1,14 @@
+import math
+
 import jax
 import jax.numpy as jnp
 from jax import lax
+from jax.experimental import pallas as pl
+from jax.experimental.pallas import tpu as pltpu
 from jax.sharding import PartitionSpec as P
 
 TURNS = 2
+VMEM = 24 << 20
 
 
 def from_behind(x, axis, by):
@@ -20,7 +25,7 @@
     return gradient + jnp.einsum("xyab,ybq->xaq", amplitude, other_rows, precision=highest)
 
 
-def per_device(raw_integrals, virtual_coeffs, metric_root, occ_energies, virt_energies):
+def any_replicas(raw_integrals, virtual_coeffs, metric_root, occ_energies, virt_energies):
     highest = lax.Precision.HIGHEST
     halfway = jnp.einsum("ipm,ma->ipa", raw_integrals, virtual_coeffs, precision=highest)
     regrouped = lax.all_to_all(halfway, "blk", split_axis=0, concat_axis=1, tiled=True)
@@ -29,13 +34,11 @@
     fitted = lax.all_gather(fitted_part, "rep", axis=2, tiled=True)
     replica = lax.axis_index("rep")
     replicas = lax.axis_size("rep")
-    turns = TURNS
-    turn_unit = 1
     travel_rows = fitted
     travel_eps = occ_energies
     for bit_index in range((replicas - 1).bit_length()):
         shifted_rows, shifted_eps = from_behind(
-            (travel_rows, travel_eps), "blk", (1 << bit_index) * turns
+            (travel_rows, travel_eps), "blk", (1 << bit_index) * TURNS
         )
         chosen = replica >> bit_index & 1 == 1
         travel_rows = jnp.where(chosen, shifted_rows, travel_rows)
@@ -45,14 +48,255 @@
     def advance(turn_index, state_now):
         other_rows, other_eps, total = state_now
         total = pair_terms(fitted, occ_energies, other_rows, other_eps, virt_energies, total)
-        other_rows, other_eps = from_behind((other_rows, other_eps), "blk", turn_unit)
+        other_rows, other_eps = from_behind((other_rows, other_eps), "blk", 1)
         return (other_rows, other_eps, total)
 
     travel_rows, travel_eps, gradient = lax.fori_loop(
-        0, turns - 1, advance, (travel_rows, travel_eps, gradient)
+        0, TURNS - 1, advance, (travel_rows, travel_eps, gradient)
     )
     gradient = pair_terms(fitted, occ_energies, travel_rows, travel_eps, virt_energies, gradient)
     return lax.psum_scatter(gradient, "rep", scatter_dimension=2, tiled=True)
+
+
+def split(x):
+    high = x.astype(jnp.bfloat16)
+    return high, (x - high.astype(jnp.float32)).astype(jnp.bfloat16)
+
+
+def product(x, y, over_x=1, over_y=0):
+    one = lambda p, q: lax.dot_general(
+        p, q, (((over_x,), (over_y,)), ((), ())), preferred_element_type=jnp.float32
+    )
+    return one(x[0], y[0]) + (one(x[0], y[1]) + one(x[1], y[0]))
+
+
+def transform_kernel(raw_ref, coeffs_ref, eps_ref, out_ref, high_ref, low_ref):
+    depth = raw_ref.shape[1]
+
+    @pl.when(pl.program_id(0) == 0)
+    def _():
+        high_ref[...], low_ref[...] = split(coeffs_ref[...])
+
+    raw = raw_ref[...].reshape(-1, raw_ref.shape[2])
+    done = product(split(raw), (high_ref[...], low_ref[...]))
+    out_ref[:, :depth] = done.reshape(raw_ref.shape[0], depth, -1)
+    out_ref[:, depth:] = jnp.full((out_ref.shape[0], 8, out_ref.shape[2]), eps_ref[0], jnp.float32)
+
+
+def fit_kernel(
+    got_ref, metric_ref, there_ref, mate_ref, out_ref, eps_ref,
+    rows_high, rows_low, square_high, square_low,
+):
+    rep = lax.axis_index("rep")
+    core = lax.axis_index("blk") % 2
+    depth = got_ref.shape[1] - 8
+    wide = metric_ref.shape[1]
+    half, step = wide // 2, wide // 4
+    rows = split(got_ref[:, :depth].reshape(-1, got_ref.shape[2]).T)
+    for part in range(2):
+        at = slice(part * wide, (part + 1) * wide)
+        rows_high[part], rows_low[part] = rows[0][:, at], rows[1][:, at]
+    out_ref[rep] = product(rows, split(metric_ref[...]))
+    for ref, which in ((there_ref, core), (mate_ref, 1 - core)):
+        for row, column, piece in (
+            (which * half, which * half, ref[:half]),
+            (which * step, half, ref[half:]),
+            (half, which * step, ref[half:].T),
+        ):
+            at = pl.ds(pl.multiple_of(row, step), piece.shape[0])
+            to = pl.ds(pl.multiple_of(column, step), piece.shape[1])
+            square_high[at, to], square_low[at, to] = split(piece)
+    mine = metric_ref[pl.ds(pl.multiple_of((1 - rep) * wide, wide), wide)]
+    out_ref[1 - rep] = product((rows_high[rep], rows_low[rep]), split(mine), 1, 1) + product(
+        (rows_high[1 - rep], rows_low[1 - rep]), (square_high[...], square_low[...])
+    )
+    eps_ref[...] = got_ref[:, depth:]
+
+
+def coulomb(own, other_ref):
+    total = 0.0
+    for half in range(2):
+        total = total + product(own[half], split(other_ref[half]), 1, 1)
+    return total
+
+
+def amplitude(whole, levels_ref, column_ref, eps_ref, index, other):
+    size = eps_ref.shape[2]
+    lower = eps_ref[index][:1] + eps_ref[other][:1]
+    across = levels_ref[...] - jnp.concatenate([lower] * (whole.shape[1] // size), 1)
+    return (2.0 * whole - whole.T) / (column_ref[...] + across)
+
+
+def gradient(weights, first_ref, second_ref):
+    rep = lax.axis_index("rep")
+    size = first_ref.shape[1]
+    weights = split(weights)
+    one = lambda at, ref: product(
+        (weights[0][:, at : at + size], weights[1][:, at : at + size]), split(ref[rep])
+    )
+    return one(0, first_ref) + one(size, second_ref)
+
+
+def own_parts(high_ref, low_ref):
+    return [(high_ref[half], low_ref[half]) for half in range(2)]
+
+
+def own_kernel(
+    fit_ref, over_ref, near_ref, mate_ref, levels_ref, column_ref, eps_ref,
+    high_ref, low_ref, near_out, mate_out, total_ref,
+):
+    size = fit_ref.shape[1]
+    for half in range(2):
+        high_ref[half, :size], low_ref[half, :size] = split(fit_ref[half])
+        high_ref[half, size:], low_ref[half, size:] = split(over_ref[half])
+    own = own_parts(high_ref, low_ref)
+    whole = 0.0
+    for half in range(2):
+        whole = whole + product(own[half], own[half], 1, 1)
+    block = lax.axis_index("blk")
+    weights = amplitude(whole, levels_ref, column_ref, eps_ref, block, block)
+    total_ref[...] = gradient(weights, fit_ref, over_ref)
+    near_out[...] = coulomb(own, near_ref)
+    mate_out[...] = coulomb(own, mate_ref)
+
+
+def behind(by):
+    blocks = lax.axis_size("blk")
+    return lax.rem(lax.axis_index("blk") + blocks - by, blocks)
+
+
+def near_kernel(
+    high_ref, low_ref, far_ref, far_over_ref, near_ref, near_over_ref, near_half_ref,
+    levels_ref, column_ref, eps_ref, sum_ref, total_ref,
+):
+    own = own_parts(high_ref, low_ref)
+    block = lax.axis_index("blk")
+    core = block % 2
+    total = sum_ref[...]
+    whole = jnp.concatenate([coulomb(own, far_ref), coulomb(own, far_over_ref)], 1)
+    weights = amplitude(whole, levels_ref, column_ref, eps_ref, block, jnp.where(core == 0, behind(3), behind(1)))
+    total = total + gradient(weights, far_ref, far_over_ref)
+    whole = jnp.concatenate([near_half_ref[...], coulomb(own, near_over_ref)], 1)
+    weights = amplitude(whole, levels_ref, column_ref, eps_ref, block, behind(2))
+    total_ref[...] = total + gradient(weights, near_ref, near_over_ref)
+
+
+def mate_kernel(
+    high_ref, low_ref, mate_ref, mate_over_ref, mate_half_ref,
+    levels_ref, column_ref, eps_ref, sum_ref, out_ref,
+):
+    own = own_parts(high_ref, low_ref)
+    rep = lax.axis_index("rep")
+    block = lax.axis_index("blk")
+    core = block % 2
+    size = mate_ref.shape[1]
+    whole = jnp.concatenate([mate_half_ref[...], coulomb(own, mate_over_ref)], 1)
+    weights = amplitude(whole, levels_ref, column_ref, eps_ref, block, jnp.where(core == 0, behind(1), behind(3)))
+    total = sum_ref[...] + gradient(weights, mate_ref, mate_over_ref)
+    out_ref[0, pl.ds(pl.multiple_of(rep * size, size), size)] = total[:size]
+    out_ref[0, pl.ds(pl.multiple_of((1 - rep) * size, size), size)] = total[size:]
+
+
+def call(kernel, out, *arrays, flops, scratch=()):
+    given = sum(a.size * a.dtype.itemsize for a in arrays)
+    made = sum(math.prod(o.shape) * o.dtype.itemsize for o in jax.tree.leaves(out))
+    vmem = pl.BlockSpec(memory_space=pltpu.VMEM)
+    return pl.pallas_call(
+        kernel,
+        out_shape=out,
+        in_specs=[vmem] * len(arrays),
+        out_specs=jax.tree.map(lambda _: vmem, out),
+        scratch_shapes=scratch,
+        cost_estimate=pl.CostEstimate(flops=flops, bytes_accessed=given + made, transcendentals=0),
+        compiler_params=pltpu.CompilerParams(vmem_limit_bytes=VMEM),
+    )(*arrays)
+
+
+def shape(*dims, dtype=jnp.float32):
+    return jax.ShapeDtypeStruct(dims, dtype)
+
+
+def two_replicas(raw_integrals, virtual_coeffs, metric_root, occ_energies, virt_energies):
+    blocks = lax.axis_size("blk")
+    block = lax.axis_index("blk")
+    rep = lax.axis_index("rep")
+    core = block % 2
+    swap = [(0, 1), (1, 0)]
+    mate = [(i, i ^ 1) for i in range(blocks)]
+    orbitals, depth, atoms = raw_integrals.shape
+    rows = virtual_coeffs.shape[1]
+    aux, wide = metric_root.shape
+    group = math.gcd(orbitals, 2)
+    base, half, step = rep * wide, wide // 2, wide // 4
+    quarter = jnp.concatenate(
+        [
+            lax.dynamic_slice(metric_root, (base + core * half, core * half), (half, half)),
+            lax.dynamic_slice(metric_root, (base + core * step, half), (step, half)),
+        ]
+    )
+    there = lax.ppermute(quarter, "rep", swap)
+    sent = pl.pallas_call(
+        transform_kernel,
+        grid=(orbitals // group,),
+        in_specs=[
+            pl.BlockSpec((group, depth, atoms), lambda i: (i, 0, 0)),
+            pl.BlockSpec((atoms, rows), lambda i: (0, 0)),
+            pl.BlockSpec(memory_space=pltpu.SMEM),
+        ],
+        out_specs=pl.BlockSpec((group, depth + 8, rows), lambda i: (i, 0, 0)),
+        out_shape=shape(orbitals, depth + 8, rows),
+        scratch_shapes=[pltpu.VMEM((atoms, rows), jnp.bfloat16)] * 2,
+        cost_estimate=pl.CostEstimate(
+            flops=6 * raw_integrals.size * rows,
+            bytes_accessed=4 * raw_integrals.size,
+            transcendentals=0,
+        ),
+        name="transform_kernel",
+    )(raw_integrals, virtual_coeffs, occ_energies)
+    got = lax.all_to_all(sent, "blk", split_axis=0, concat_axis=0, tiled=True)
+    there_mate = lax.ppermute(there, "blk", mate)
+    fit, eps = call(
+        fit_kernel,
+        (shape(2, rows, wide), shape(blocks, 8, rows)),
+        got, metric_root, there, there_mate,
+        flops=6 * aux * aux * rows,
+        scratch=[pltpu.VMEM((2, rows, wide), jnp.bfloat16)] * 2
+        + [pltpu.VMEM((wide, wide), jnp.bfloat16)] * 2,
+    )
+    over = lax.ppermute(fit, "rep", swap)
+    near = from_behind(fit, "blk", 2)
+    fit_late, over = lax.optimization_barrier((fit, over))
+    past = [(i, (i + 1 + 2 * (i % 2)) % blocks) for i in range(blocks)]
+    far_over = lax.ppermute(over, "blk", past)
+    far = lax.ppermute(fit_late, "blk", past)
+    near_over = lax.ppermute(near, "rep", swap)
+    near_mate = lax.ppermute(near, "blk", mate)
+    levels = jnp.where(rep == 0, virt_energies, jnp.roll(virt_energies, rows))
+    levels = (levels[None, :], levels[:, None])
+    both = 2 * rows
+    halves = shape(2, both, wide, dtype=jnp.bfloat16)
+    pair = 6 * both * rows * aux
+    high, low, near_half, mate_half, total = call(
+        own_kernel,
+        (halves, halves, shape(both, rows), shape(both, rows), shape(both, wide)),
+        fit_late, over, near, near_mate, *levels, eps, flops=5 * pair,
+    )
+    mate_over = lax.ppermute(near_over, "blk", mate)
+    total = call(
+        near_kernel, shape(both, wide), high, low, far, far_over, near, near_over,
+        near_half, *levels, eps, total, flops=5 * pair,
+    )
+    return call(
+        mate_kernel, shape(1, both, wide), high, low, near_mate, mate_over, mate_half,
+        *levels, eps, total, flops=2 * pair,
+    )
+
+
+def per_device(*arrays):
+    blocks = lax.axis_size("blk")
+    if lax.axis_size("rep") == 2 and TURNS == 2 and blocks % 2 == 0 and arrays[3].shape == (1,):
+        return two_replicas(*arrays)
+    return any_replicas(*arrays)
 
 
 def solution(mesh):

time: 166 us -> 73.2 us (0.44)
  waiting for transfers between devices: 91.4 us -> 40.1 us
  blocking collectives: 21.6 us -> 0 us
  matrix products: 19 us -> 0 us
  Pallas kernels: 0 us -> 18.5 us
  between operations: 14.6 us -> 0.95 us
  local copies, waits for them, and re-layouts: 3.58 us -> 0.19 us
  other arithmetic: 2.4 us -> 0.04 us
    all_gather x2 -> x0, waiting for transfers between devices: 42.3 us -> none  [the longest x1 21.4 us: per_device(): fitted = lax.all_gather(fitted_part, 'rep', axis=2, tiled=True)]
    ppermute x0 -> x8, waiting for transfers between devices: none -> 23.2 us  [the longest x1 11.2 us: two_replicas(): near_over = lax.ppermute(near, 'rep', swap)]
    all_to_all x1 -> x0, blocking collectives: 21.6 us -> none  [per_device(): lax.all_to_all(halfway, 'blk', split_axis=0, concat_axis=1, tiled=True)]
    dot_general x6 -> x0, matrix products: 19 us -> none  [the longest x2 6.38 us: pair_terms(): jnp.einsum('xyab,ybq->xaq', amplitude, other_rows, precision=highest)]
    pallas_call x0 -> x5, Pallas kernels: none -> 18.5 us  [the longest x4 12.2 us: call(): pl.pallas_call(kernel, out_shape=out, in_specs=[vmem] * len(arrays), out_...]
    reduce_scatter x1 -> x0, waiting for transfers between devices: 17.1 us -> none  [per_device(): return lax.psum_scatter(gradient, 'rep', scatter_dimension=2, tiled=True)]
    ppermute x4 -> x1, waiting for transfers between devices: 31.9 us -> 14.9 us  [from_behind(): return lax.ppermute(x, axis, [(i, (i + by) % count) for i in range(count)])]
    ppermute x4 -> x1, starting transfers between devices: 13.3 us -> 0.62 us  [from_behind(): return lax.ppermute(x, axis, [(i, (i + by) % count) for i in range(count)])]
  transfers between devices with their start and end apart: 7 -> 10, of which waited for: 5 -> 6; matrix products, arithmetic and copies ran while one was open for 4% -> 0% of each run, Pallas kernels for 0% -> 10%
where the time goes in v2:
time: 73.2 us; the launch traced here: 72.9 us
  waiting for transfers between devices  40.1 us (55%)
  Pallas kernels  18.5 us (25%)
  starting transfers between devices  13.1 us (18%)
  between operations  0.95 us (1%)
    ppermute x1, waiting for transfers between devices, from_behind(): return lax.ppermute(x, axis, [(i, (i + by) % count) for i in range(count)])  14.9 us
    pallas_call x4, Pallas kernels, call(): pl.pallas_call(kernel, out_shape=out, in_specs=[vmem] * len(arrays), out_...  12.2 us
    ppermute x1, waiting for transfers between devices, two_replicas(): near_over = lax.ppermute(near, 'rep', swap)  11.2 us
    ppermute x1, waiting for transfers between devices, two_replicas(): there = lax.ppermute(quarter, 'rep', swap)  9.91 us
    all_to_all x1, starting transfers between devices, two_replicas(): got = lax.all_to_all(sent, 'blk', split_axis=0, concat_axis=0, tiled=True)  7.41 us
    pallas_call x1, Pallas kernels, two_replicas(): pl.pallas_call(transform_kernel, grid=(orbitals // group,), in_specs=[pl....  6.32 us
    all_to_all x1, waiting for transfers between devices, two_replicas(): got = lax.all_to_all(sent, 'blk', split_axis=0, concat_axis=0, tiled=True)  2.04 us
    ppermute x1, waiting for transfers between devices, two_replicas(): there_mate = lax.ppermute(there, 'blk', mate)  1.72 us
  transfers between devices with their start and end apart: 10, of which 6 were waited for; matrix products, arithmetic and copies ran while one was open for 0% of the time, Pallas kernels for 10%

profile of v2, /device:TPU:0, one launch (start us, length us, event | category | flops | bytes accessed | tf_op | source)
XLA Modules:
  0.0 72.9 jit_solution(6935405014536368427)
XLA Ops:
  0.0 0.0 copy-start
  0.8 6.3 %transform_kernel.1 = f32[16,72,128]{2,1,0:T(8,128)} custom-call(f32[16,64,512]{2,1,0:T(8,128)} %raw_ref.1, f32[512,128]{1,0:T(8,128)} %coeffs_ref.1, f32[1]{0:T(128)S(6)} %copy.9.eps_ref), custom_call_target="tpu_custom_call" | custom-call | flops 402653184 | bytes 2097152 | tf_op jit(solution)/shard_map/transform_kernel/pallas_call | solution.py:238
  7.1 7.4 %all-to-all-start = ((f32[16,72,128]{2,1,0:T(8,128)}), f32[16,72,128]{2,1,0:T(8,128)S(1)}, u32[]{:S(2)}, u32[]{:S(2)}) async-start(f32[16,72,128]{2,1,0:T(8,128)} %transform_kernel.1), calls=%async_computation | async-start | bytes 1179648 | tf_op jit(solution)/shard_map/all_to_all | solution.py:256
  14.6 0.0 copy-done
  14.6 0.0 copy-start.1
  14.7 1.6 %collective-permute-start = (f32[384,256]{1,0:T(8,128)S(1)}, f32[384,256]{1,0:T(8,128)S(1)}, u32[]{:S(2)}, u32[]{:S(2)}) collective-permute-start(f32[384,256]{1,0:T(8,128)S(1)} %pad_maximum_fusion), channel_id=1, source_target_pairs={{0,1},{1,0},{2,3},{3,2},{4,5},{5,4},{6,7},{7,6},{8,9},{9,8},{10,11... | collective-permute-start | bytes 1179656 | tf_op jit(solution)/shard_map/ppermute | solution.py:237
  16.2 9.9 %collective-permute-done.there_ref = f32[384,256]{1,0:T(8,128)S(1)} collective-permute-done((f32[384,256]{1,0:T(8,128)S(1)}, f32[384,256]{1,0:T(8,128)S(1)}, u32[]{:S(2)}, u32[]{:S(2)}) %collective-permute-start) | collective-permute-done | bytes 393248 | tf_op jit(solution)/shard_map/ppermute | solution.py:237
  26.2 0.0 collective-permute-start.1
  26.2 1.7 %collective-permute-done.1.mate_ref = f32[384,256]{1,0:T(8,128)S(1)} collective-permute-done((f32[384,256]{1,0:T(8,128)S(1)}, f32[384,256]{1,0:T(8,128)S(1)}, u32[]{:S(2)}, u32[]{:S(2)}) %collective-permute-start.1) | collective-permute-done | bytes 393248 | tf_op jit(solution)/shard_map/ppermute | solution.py:257
  27.9 2.0 %all-to-all-done.got_ref = f32[16,72,128]{2,1,0:T(8,128)S(1)} async-done(((f32[16,72,128]{2,1,0:T(8,128)}), f32[16,72,128]{2,1,0:T(8,128)S(1)}, u32[]{:S(2)}, u32[]{:S(2)}) %all-to-all-start) | async-done | bytes 589856 | tf_op jit(solution)/shard_map/all_to_all | solution.py:256
  29.9 2.3 %shard_map.55 = (f32[2,128,512]{2,1,0:T(8,128)}, f32[16,8,128]{2,1,0:T(8,128)S(1)}) custom-call(f32[16,72,128]{2,1,0:T(8,128)S(1)} %all-to-all-done.got_ref, f32[1024,512]{1,0:T(8,128)S(1)} %copy-done, f32[384,256]{1,0:T(8,128)S(1)} %collective-permute-done.there_ref, f32[384,256]{1,0:T(8,128)S(1)} %collective-permute-done.1.mate_ref), custom_call_target="tpu_custom_call" | custom-call | flops 805306368 | bytes 4063232 | tf_op jit(solution)/shard_map/pallas_call | solution.py:204
  32.2 0.6 collective-permute-start.3
  32.8 1.5 %collective-permute-start.2 = (f32[2,128,512]{2,1,0:T(8,128)}, f32[2,128,512]{2,1,0:T(8,128)}, u32[]{:S(2)}, u32[]{:S(2)}) collective-permute-start(f32[2,128,512]{2,1,0:T(8,128)} %get-tuple-element.15.fit_ref), channel_id=1, source_target_pairs={{0,1},{1,0},{2,3},{3,2},{4,5},{5,4},{6,7},{7,6},{8,9},{9,8},{10,11... | collective-permute-start | bytes 1572872 | tf_op jit(solution)/shard_map/ppermute | solution.py:266
  34.3 14.9 %collective-permute-done.3.near_ref = f32[2,128,512]{2,1,0:T(8,128)S(1)} collective-permute-done((f32[2,128,512]{2,1,0:T(8,128)}, f32[2,128,512]{2,1,0:T(8,128)S(1)}, u32[]{:S(2)}, u32[]{:S(2)}) %collective-permute-start.3) | collective-permute-done | bytes 524320 | tf_op jit(solution)/shard_map/ppermute | solution.py:16
  49.2 1.5 %collective-permute-start.5 = (f32[2,128,512]{2,1,0:T(8,128)S(1)}, f32[2,128,512]{2,1,0:T(8,128)S(1)}, u32[]{:S(2)}, u32[]{:S(2)}) collective-permute-start(f32[2,128,512]{2,1,0:T(8,128)S(1)} %collective-permute-done.3.near_ref), channel_id=1, source_target_pairs={{0,1},{1,0},{2,3},{3,2},{4,5},{5,4},{6,7},{7,6},{8,9},{9,8},{10,11... | collective-permute-start | bytes 1572872 | tf_op jit(solution)/shard_map/ppermute | solution.py:272
  50.7 0.0 collective-permute-start.4
  50.7 0.0 collective-permute-done.2.over_ref
  50.7 0.5 collective-permute-start.7
  51.2 0.0 collective-permute-start.8
  51.2 11.2 %collective-permute-done.5.near_over_ref = f32[2,128,512]{2,1,0:T(8,128)S(1)} collective-permute-done((f32[2,128,512]{2,1,0:T(8,128)S(1)}, f32[2,128,512]{2,1,0:T(8,128)S(1)}, u32[]{:S(2)}, u32[]{:S(2)}) %collective-permute-start.5) | collective-permute-done | bytes 524320 | tf_op jit(solution)/shard_map/ppermute | solution.py:272
  62.4 0.0 collective-permute-start.6
  62.4 0.0 copy-done.1
  62.5 0.1 copy.6.column_ref
  62.6 0.0 collective-permute-done.4.mate_ref
  62.6 4.0 %shard_map.56 = (bf16[2,256,512]{2,1,0:T(8,128)(2,1)S(1)}, bf16[2,256,512]{2,1,0:T(8,128)(2,1)S(1)}, f32[256,128]{1,0:T(8,128)S(1)}, f32[256,128]{1,0:T(8,128)S(1)}, f32[256,512]{1,0:T(8,128)S(1)}) custom-call(f32[2,128,512]{2,1,0:T(8,128)} %get-tuple-element.15.fit_ref, f32[2,128,512]{2,1,0:T(8,128)} %collective-permute-done.2.over_ref, ...), custom_call_target="tpu_custom_call" | custom-call | flops 1006632960 | bytes 3999744 | tf_op jit(solution)/shard_map/pallas_call | solution.py:204
  66.6 0.0 collective-permute-done.7.far_ref
  66.6 0.3 collective-permute-done.8.far_over_ref
  66.9 3.2 %shard_map.57.sum_ref = f32[256,512]{1,0:T(8,128)S(1)} custom-call(bf16[2,256,512]{2,1,0:T(8,128)(2,1)S(1)} %get-tuple-element.18.high_ref, bf16[2,256,512]{2,1,0:T(8,128)(2,1)S(1)} %get-tuple-element.19.low_ref, f32[2,128,512]{2,1,0:T(8,128)S(1)} %collective-permute-done.7.far_ref, f32[2,128,512]{2,1,0:T(8,128)S(1)} %collective-permute-done.8.far_over_ref, ...), custom_call_target="tpu_custom_call" | custom-call | flops 1006632960 | bytes 4392960 | tf_op jit(solution)/shard_map/pallas_call | solution.py:204
  70.2 0.0 collective-permute-done.6.mate_over_ref
  70.2 2.7 %shard_map.58 = f32[1,256,512]{2,1,0:T(8,128)} custom-call(bf16[2,256,512]{2,1,0:T(8,128)(2,1)S(1)} %get-tuple-element.18.high_ref, bf16[2,256,512]{2,1,0:T(8,128)(2,1)S(1)} %get-tuple-element.19.low_ref, f32[2,128,512]{2,1,0:T(8,128)S(1)} %collective-permute-done.4.mate_ref, f32[2,128,512]{2,1,0:T(8,128)S(1)} %collective-permute-done.6.mate_over_ref, ...), custom_call_target="tpu_custom_call" | custom-call | flops 402653184 | bytes 3344384 | tf_op jit(solution)/shard_map/pallas_call | solution.py:204
  (5 shorter events, 0.1 us)
Async XLA Ops:
  0.0 14.6 %copy-start = (f32[1024,512]{1,0:T(8,128)S(1)}, f32[1024,512]{1,0:T(8,128)}, u32[]{:S(2)}) copy-start(f32[1024,512]{1,0:T(8,128)} %metric_ref.1) | copy-start | bytes 6291460
  7.1 22.8 %all-to-all-start = ((f32[16,72,128]{2,1,0:T(8,128)}), f32[16,72,128]{2,1,0:T(8,128)S(1)}, u32[]{:S(2)}, u32[]{:S(2)}) async-start(f32[16,72,128]{2,1,0:T(8,128)} %transform_kernel.1), calls=%async_computation | async-start | bytes 1179648 | tf_op jit(solution)/shard_map/all_to_all | solution.py:256
  14.6 47.8 %copy-start.1 = (f32[256]{0:T(256)S(1)}, f32[256]{0:T(256)}, u32[]{:S(2)}) copy-start(f32[256]{0:T(256)} %param.9) | copy-start | bytes 3076
  14.7 11.5 %collective-permute-start = (f32[384,256]{1,0:T(8,128)S(1)}, f32[384,256]{1,0:T(8,128)S(1)}, u32[]{:S(2)}, u32[]{:S(2)}) collective-permute-start(f32[384,256]{1,0:T(8,128)S(1)} %pad_maximum_fusion), channel_id=1, source_target_pairs={{0,1},{1,0},{2,3},{3,2},{4,5},{5,4},{6,7},{7,6},{8,9},{9,8},{10,11... | collective-permute-start | bytes 1179656 | tf_op jit(solution)/shard_map/ppermute | solution.py:237
  26.2 1.7 %collective-permute-start.1 = (f32[384,256]{1,0:T(8,128)S(1)}, f32[384,256]{1,0:T(8,128)S(1)}, u32[]{:S(2)}, u32[]{:S(2)}) collective-permute-start(f32[384,256]{1,0:T(8,128)S(1)} %collective-permute-done.there_ref), channel_id=1, source_target_pairs={{0,2},{2,0},{4,6},{6,4},{8,10},{10,8},{12,14},{14,12},{16,18},{18,... | collective-permute-start | bytes 1179656 | tf_op jit(solution)/shard_map/ppermute | solution.py:257
  32.2 17.0 %collective-permute-start.3 = (f32[2,128,512]{2,1,0:T(8,128)}, f32[2,128,512]{2,1,0:T(8,128)S(1)}, u32[]{:S(2)}, u32[]{:S(2)}) collective-permute-start(f32[2,128,512]{2,1,0:T(8,128)} %get-tuple-element.15.fit_ref), channel_id=1, source_target_pairs={{0,4},{2,6},{4,8},{6,10},{8,12},{10,14},{12,16},{14,18},{16,20},{1... | collective-permute-start | bytes 1572872 | tf_op jit(solution)/shard_map/ppermute | solution.py:16
  32.8 17.9 %collective-permute-start.2 = (f32[2,128,512]{2,1,0:T(8,128)}, f32[2,128,512]{2,1,0:T(8,128)}, u32[]{:S(2)}, u32[]{:S(2)}) collective-permute-start(f32[2,128,512]{2,1,0:T(8,128)} %get-tuple-element.15.fit_ref), channel_id=1, source_target_pairs={{0,1},{1,0},{2,3},{3,2},{4,5},{5,4},{6,7},{7,6},{8,9},{9,8},{10,11... | collective-permute-start | bytes 1572872 | tf_op jit(solution)/shard_map/ppermute | solution.py:266
  49.2 13.2 %collective-permute-start.5 = (f32[2,128,512]{2,1,0:T(8,128)S(1)}, f32[2,128,512]{2,1,0:T(8,128)S(1)}, u32[]{:S(2)}, u32[]{:S(2)}) collective-permute-start(f32[2,128,512]{2,1,0:T(8,128)S(1)} %collective-permute-done.3.near_ref), channel_id=1, source_target_pairs={{0,1},{1,0},{2,3},{3,2},{4,5},{5,4},{6,7},{7,6},{8,9},{9,8},{10,11... | collective-permute-start | bytes 1572872 | tf_op jit(solution)/shard_map/ppermute | solution.py:272
  50.7 11.9 %collective-permute-start.4 = (f32[2,128,512]{2,1,0:T(8,128)S(1)}, f32[2,128,512]{2,1,0:T(8,128)S(1)}, u32[]{:S(2)}, u32[]{:S(2)}) collective-permute-start(f32[2,128,512]{2,1,0:T(8,128)S(1)} %collective-permute-done.3.near_ref), channel_id=1, source_target_pairs={{0,2},{2,0},{4,6},{6,4},{8,10},{10,8},{12,14},{14,12},{16,18},{18,... | collective-permute-start | bytes 1572872 | tf_op jit(solution)/shard_map/ppermute | solution.py:273
  50.7 15.9 %collective-permute-start.7 = (f32[2,128,512]{2,1,0:T(8,128)}, f32[2,128,512]{2,1,0:T(8,128)S(1)}, u32[]{:S(2)}, u32[]{:S(2)}) collective-permute-start(f32[2,128,512]{2,1,0:T(8,128)} %get-tuple-element.15.fit_ref), channel_id=1, source_target_pairs={{0,2},{2,8},{4,6},{6,12},{8,10},{10,16},{12,14},{14,20},{16,18},{1... | collective-permute-start | bytes 1572872 | tf_op jit(solution)/shard_map/ppermute | solution.py:271
  51.2 15.7 %collective-permute-start.8 = (f32[2,128,512]{2,1,0:T(8,128)}, f32[2,128,512]{2,1,0:T(8,128)S(1)}, u32[]{:S(2)}, u32[]{:S(2)}) collective-permute-start(f32[2,128,512]{2,1,0:T(8,128)} %collective-permute-done.2.over_ref), channel_id=1, source_target_pairs={{0,2},{2,8},{4,6},{6,12},{8,10},{10,16},{12,14},{14,20},{16,18},{1... | collective-permute-start | bytes 1572872 | tf_op jit(solution)/shard_map/ppermute | solution.py:270
  62.4 7.8 %collective-permute-start.6 = (f32[2,128,512]{2,1,0:T(8,128)S(1)}, f32[2,128,512]{2,1,0:T(8,128)S(1)}, u32[]{:S(2)}, u32[]{:S(2)}) collective-permute-start(f32[2,128,512]{2,1,0:T(8,128)S(1)} %collective-permute-done.5.near_over_ref), channel_id=1, source_target_pairs={{0,2},{2,0},{4,6},{6,4},{8,10},{10,8},{12,14},{14,12},{16,18},{18,... | collective-permute-start | bytes 1572872 | tf_op jit(solution)/shard_map/ppermute | solution.py:284

commit v3 on v2

v3 whole, which is shorter than its diff:
```python
import math

import jax
import jax.numpy as jnp
from jax import lax
from jax.experimental import pallas as pl
from jax.experimental.pallas import tpu as pltpu
from jax.sharding import PartitionSpec as P

TURNS = 2
VMEM = 24 << 20


def from_behind(x, axis, by):
    count = lax.axis_size(axis)
    return lax.ppermute(x, axis, [(i, (i + by) % count) for i in range(count)])


def pair_terms(own_rows, own_eps, other_rows, other_eps, virt_energies, gradient):
    highest = lax.Precision.HIGHEST
    coulomb = jnp.einsum("xaq,ybq->xyab", own_rows, other_rows, precision=highest)
    spread = virt_energies[:, None] + virt_energies[None, :]
    denominator = spread[None, None] - own_eps[:, None, None, None] - other_eps[None, :, None, None]
    amplitude = (2.0 * coulomb - jnp.swapaxes(coulomb, 2, 3)) / denominator
    return gradient + jnp.einsum("xyab,ybq->xaq", amplitude, other_rows, precision=highest)


def any_replicas(raw_integrals, virtual_coeffs, metric_root, occ_energies, virt_energies):
    highest = lax.Precision.HIGHEST
    halfway = jnp.einsum("ipm,ma->ipa", raw_integrals, virtual_coeffs, precision=highest)
    regrouped = lax.all_to_all(halfway, "blk", split_axis=0, concat_axis=1, tiled=True)
    complete = lax.all_gather(regrouped, "rep", axis=2, tiled=True)
    fitted_part = jnp.einsum("xpa,pq->xaq", complete, metric_root, precision=highest)
    fitted = lax.all_gather(fitted_part, "rep", axis=2, tiled=True)
    replica = lax.axis_index("rep")
    replicas = lax.axis_size("rep")
    travel_rows = fitted
    travel_eps = occ_energies
    for bit_index in range((replicas - 1).bit_length()):
        shifted_rows, shifted_eps = from_behind(
            (travel_rows, travel_eps), "blk", (1 << bit_index) * TURNS
        )
        chosen = replica >> bit_index & 1 == 1
        travel_rows = jnp.where(chosen, shifted_rows, travel_rows)
        travel_eps = jnp.where(chosen, shifted_eps, travel_eps)
    gradient = jnp.zeros(fitted.shape, jnp.float32)

    def advance(turn_index, state_now):
        other_rows, other_eps, total = state_now
        total = pair_terms(fitted, occ_energies, other_rows, other_eps, virt_energies, total)
        other_rows, other_eps = from_behind((other_rows, other_eps), "blk", 1)
        return (other_rows, other_eps, total)

    travel_rows, travel_eps, gradient = lax.fori_loop(
        0, TURNS - 1, advance, (travel_rows, travel_eps, gradient)
    )
    gradient = pair_terms(fitted, occ_energies, travel_rows, travel_eps, virt_energies, gradient)
    return lax.psum_scatter(gradient, "rep", scatter_dimension=2, tiled=True)


def split(x):
    high = x.astype(jnp.bfloat16)
    return high, (x - high.astype(jnp.float32)).astype(jnp.bfloat16)


def product(x, y, over_x=1, over_y=0):
    one = lambda p, q: lax.dot_general(
        p, q, (((over_x,), (over_y,)), ((), ())), preferred_element_type=jnp.float32
    )
    return one(x[0], y[0]) + (one(x[0], y[1]) + one(x[1], y[0]))


def transform_kernel(
    raw_hbm, coeffs_hbm, eps_ref, out_hbm, raw_ref, coeffs_ref, out_ref, coeffs_sem, in_sems, out_sems
):
    steps = in_sems.shape[0]
    group = raw_ref.shape[0] // steps
    depth, rows = raw_ref.shape[1], coeffs_ref.shape[1]
    parts = [pl.ds(step * group, group) for step in range(steps)]
    first = pltpu.make_async_copy(coeffs_hbm, coeffs_ref, coeffs_sem)
    first.start()
    into = [
        pltpu.make_async_copy(raw_hbm.at[at], raw_ref.at[at], in_sems.at[step])
        for step, at in enumerate(parts)
    ]
    out = [
        pltpu.make_async_copy(out_ref.at[at], out_hbm.at[at], out_sems.at[step])
        for step, at in enumerate(parts)
    ]
    for copy in into:
        copy.start()
    out_ref[:, depth:] = jnp.full((out_ref.shape[0], 8, rows), eps_ref[0], jnp.float32)
    first.wait()
    high, low = split(coeffs_ref[...])
    both = jnp.concatenate([high, low], 1)
    one = lambda x, y: lax.dot_general(
        x, y, (((1,), (0,)), ((), ())), preferred_element_type=jnp.float32
    )
    for step, at in enumerate(parts):
        into[step].wait()
        raw = split(raw_ref[at].reshape(group * depth, -1))
        wide = one(raw[0], both)
        done = wide[:, :rows] + (wide[:, rows:] + one(raw[1], high))
        out_ref[at, :depth] = done.reshape(group, depth, rows)
        out[step].start()
    for copy in out:
        copy.wait()


def fit_kernel(
    got_ref, metric_ref, there_ref, mate_ref, out_ref, first_ref, second_ref, eps_ref,
    rows_high, rows_low, square_high, square_low,
):
    rep = lax.axis_index("rep")
    core = lax.axis_index("blk") % 2
    depth = got_ref.shape[1] - 8
    wide = metric_ref.shape[1]
    half, step = wide // 2, wide // 4
    rows = split(got_ref[:, :depth].reshape(-1, got_ref.shape[2]).T)
    for part in range(2):
        at = slice(part * wide, (part + 1) * wide)
        rows_high[part], rows_low[part] = rows[0][:, at], rows[1][:, at]
    mine = product(rows, split(metric_ref[...]))
    for ref, which in ((there_ref, core), (mate_ref, 1 - core)):
        for row, column, piece in (
            (which * half, which * half, ref[:half]),
            (which * step, half, ref[half:]),
            (half, which * step, ref[half:].T),
        ):
            at = pl.ds(pl.multiple_of(row, step), piece.shape[0])
            to = pl.ds(pl.multiple_of(column, step), piece.shape[1])
            square_high[at, to], square_low[at, to] = split(piece)
    from_rows = metric_ref[pl.ds(pl.multiple_of((1 - rep) * wide, wide), wide)]
    there = product((rows_high[rep], rows_low[rep]), split(from_rows), 1, 1) + product(
        (rows_high[1 - rep], rows_low[1 - rep]), (square_high[...], square_low[...])
    )
    first_ref[...] = jnp.where(rep == 0, mine, there)
    second_ref[...] = jnp.where(rep == 0, there, mine)
    out_ref[rep] = mine
    out_ref[1 - rep] = there
    eps_ref[...] = got_ref[:, depth:]


def beside(own, others):
    other = split(jnp.concatenate(others, 0))
    count = other[0].shape[0]
    if count == own[0].shape[0]:
        return product(own, other, 1, 1)
    one = lambda x, y: lax.dot_general(
        x, y, (((1,), (1,)), ((), ())), preferred_element_type=jnp.float32
    )
    wide = one(own[0], jnp.concatenate(other, 0))
    return wide[:, :count] + (wide[:, count:] + one(own[1], other[0]))


def amplitude(whole, levels_ref, column_ref, eps_ref, index, other):
    size = eps_ref.shape[2]
    lower = eps_ref[index][:1] + eps_ref[other][:1]
    across = levels_ref[...] - jnp.concatenate([lower] * (whole.shape[1] // size), 1)
    return (2.0 * whole - whole.T) / (column_ref[...] + across)


def gradient(weights, first, second):
    return product(split(weights), split(jnp.concatenate([first, second], 0)))


def half_here(first_ref, second_ref):
    return jnp.where(lax.axis_index("rep") == 0, first_ref[...], second_ref[...])


def own_parts(high_ref, low_ref):
    return [(high_ref[half], low_ref[half]) for half in range(2)]


def own_kernel(
    fit_ref, over_ref, near0_ref, near1_ref, mate0_ref, mate1_ref, levels_ref, column_ref, eps_ref,
    high_ref, low_ref, halves_ref, total_ref,
):
    size = fit_ref.shape[1]
    rep = lax.axis_index("rep")
    for half in range(2):
        high_ref[half, :size], low_ref[half, :size] = split(fit_ref[half])
        high_ref[half, size:], low_ref[half, size:] = split(over_ref[half])
    own = own_parts(high_ref, low_ref)
    whole = product(own[0], own[0], 1, 1) + product(own[1], own[1], 1, 1)
    block = lax.axis_index("blk")
    weights = amplitude(whole, levels_ref, column_ref, eps_ref, block, block)
    total_ref[...] = gradient(weights, fit_ref[rep], over_ref[rep])
    halves_ref[...] = beside(own[0], [near0_ref[...], mate0_ref[...]]) + beside(
        own[1], [near1_ref[...], mate1_ref[...]]
    )


def over_kernel(high_ref, low_ref, near_over_ref, mate_over_ref, halves_ref):
    own = (high_ref[0], low_ref[0])
    halves_ref[...] = beside(own, [near_over_ref[...], mate_over_ref[...]])


def behind(by):
    blocks = lax.axis_size("blk")
    return lax.rem(lax.axis_index("blk") + blocks - by, blocks)


def near_kernel(
    high_ref, low_ref, near0_ref, near1_ref, over0_ref, over1_ref, halves_ref, over_halves_ref,
    levels_ref, column_ref, eps_ref, sum_ref, total_ref,
):
    size = near0_ref.shape[0]
    late = over_halves_ref[:, :size] + beside((high_ref[1], low_ref[1]), [over1_ref[...]])
    whole = jnp.concatenate([halves_ref[:, :size], late], 1)
    block = lax.axis_index("blk")
    weights = amplitude(whole, levels_ref, column_ref, eps_ref, block, behind(2))
    total_ref[...] = sum_ref[...] + gradient(
        weights, half_here(near0_ref, near1_ref), half_here(over0_ref, over1_ref)
    )


def mate_kernel(
    high_ref, low_ref, mate0_ref, mate1_ref, over0_ref, over1_ref, halves_ref, over_halves_ref,
    levels_ref, column_ref, eps_ref, sum_ref, total_ref,
):
    size = mate0_ref.shape[0]
    late = over_halves_ref[:, size:] + beside((high_ref[1], low_ref[1]), [over1_ref[...]])
    whole = jnp.concatenate([halves_ref[:, size:], late], 1)
    block = lax.axis_index("blk")
    other = jnp.where(block % 2 == 0, behind(1), behind(3))
    weights = amplitude(whole, levels_ref, column_ref, eps_ref, block, other)
    total_ref[...] = sum_ref[...] + gradient(
        weights, half_here(mate0_ref, mate1_ref), half_here(over0_ref, over1_ref)
    )


def far_kernel(
    high_ref, low_ref, far_ref, far_over_ref, levels_ref, column_ref, eps_ref, sum_ref, out_ref,
):
    own = own_parts(high_ref, low_ref)
    rep = lax.axis_index("rep")
    size = far_ref.shape[1]
    whole = beside(own[0], [far_ref[0], far_over_ref[0]]) + beside(
        own[1], [far_ref[1], far_over_ref[1]]
    )
    block = lax.axis_index("blk")
    other = jnp.where(block % 2 == 0, behind(3), behind(1))
    weights = amplitude(whole, levels_ref, column_ref, eps_ref, block, other)
    total = sum_ref[...] + gradient(weights, far_ref[rep], far_over_ref[rep])
    out_ref[0, pl.ds(pl.multiple_of(rep * size, size), size)] = total[:size]
    out_ref[0, pl.ds(pl.multiple_of((1 - rep) * size, size), size)] = total[size:]


def call(kernel, out, *arrays, flops, scratch=()):
    given = sum(a.size * a.dtype.itemsize for a in arrays)
    made = sum(math.prod(o.shape) * o.dtype.itemsize for o in jax.tree.leaves(out))
    vmem = pl.BlockSpec(memory_space=pltpu.VMEM)
    return pl.pallas_call(
        kernel,
        out_shape=out,
        in_specs=[vmem] * len(arrays),
        out_specs=jax.tree.map(lambda _: vmem, out),
        scratch_shapes=scratch,
        cost_estimate=pl.CostEstimate(flops=flops, bytes_accessed=given + made, transcendentals=0),
        compiler_params=pltpu.CompilerParams(vmem_limit_bytes=VMEM),
    )(*arrays)


def shape(*dims, dtype=jnp.float32):
    return jax.ShapeDtypeStruct(dims, dtype)


def two_replicas(raw_integrals, virtual_coeffs, metric_root, occ_energies, virt_energies):
    blocks = lax.axis_size("blk")
    block = lax.axis_index("blk")
    rep = lax.axis_index("rep")
    core = block % 2
    swap = [(0, 1), (1, 0)]
    mate = [(i, i ^ 1) for i in range(blocks)]
    orbitals, depth, _ = raw_integrals.shape
    rows = virtual_coeffs.shape[1]
    aux, wide = metric_root.shape
    steps = math.gcd(orbitals, 8)
    anywhere = pl.BlockSpec(memory_space=pl.ANY)
    sent = pl.pallas_call(
        transform_kernel,
        in_specs=[anywhere, anywhere, pl.BlockSpec(memory_space=pltpu.SMEM)],
        out_specs=anywhere,
        out_shape=shape(orbitals, depth + 8, rows),
        scratch_shapes=[
            pltpu.VMEM(raw_integrals.shape, jnp.float32),
            pltpu.VMEM(virtual_coeffs.shape, jnp.float32),
            pltpu.VMEM((orbitals, depth + 8, rows), jnp.float32),
            pltpu.SemaphoreType.DMA,
            pltpu.SemaphoreType.DMA((steps,)),
            pltpu.SemaphoreType.DMA((steps,)),
        ],
        cost_estimate=pl.CostEstimate(
            flops=6 * raw_integrals.size * rows,
            bytes_accessed=4 * raw_integrals.size,
            transcendentals=0,
        ),
        name="transform_kernel",
    )(raw_integrals, virtual_coeffs, occ_energies)
    base, half, step = rep * wide, wide // 2, wide // 4
    quarter = jnp.concatenate(
        [
            lax.dynamic_slice(metric_root, (base + core * half, core * half), (half, half)),
            lax.dynamic_slice(metric_root, (base + core * step, half), (step, half)),
        ]
    )
    there = lax.ppermute(quarter, "rep", swap)
    got = lax.all_to_all(sent, "blk", split_axis=0, concat_axis=0, tiled=True)
    there_mate = lax.ppermute(there, "blk", mate)
    piece = shape(rows, wide)
    fit, first, second, eps = call(
        fit_kernel,
        (shape(2, rows, wide), piece, piece, shape(blocks, 8, rows)),
        got, metric_root, there, there_mate,
        flops=6 * aux * aux * rows,
        scratch=[pltpu.VMEM((2, rows, wide), jnp.bfloat16)] * 2
        + [pltpu.VMEM((wide, wide), jnp.bfloat16)] * 2,
    )
    past = [(i, (i + 1 + 2 * (i % 2)) % blocks) for i in range(blocks)]
    near0 = from_behind(first, "blk", 2)
    over = lax.ppermute(fit, "rep", swap)
    near1 = from_behind(second, "blk", 2)
    near_over0 = lax.ppermute(near0, "rep", swap)
    far = lax.ppermute(fit, "blk", past)
    far_over = lax.ppermute(over, "blk", past)
    near_over1 = lax.ppermute(near1, "rep", swap)
    mate0 = lax.ppermute(near0, "blk", mate)
    mate1 = lax.ppermute(near1, "blk", mate)
    levels = jnp.where(rep == 0, virt_energies, jnp.roll(virt_energies, rows))
    levels = (levels[None, :], levels[:, None])
    both = 2 * rows
    parts = shape(2, both, wide, dtype=jnp.bfloat16)
    pair = 6 * both * rows * aux
    high, low, halves, total = call(
        own_kernel,
        (parts, parts, shape(both, both), shape(both, wide)),
        fit, over, near0, near1, mate0, mate1, *levels, eps, flops=5 * pair,
    )
    mate_over0 = lax.ppermute(near_over0, "blk", mate)
    over_halves = call(
        over_kernel, shape(both, both), high, low, near_over0, mate_over0, flops=pair
    )
    mate_over1 = lax.ppermute(near_over1, "blk", mate)
    total = call(
        near_kernel, shape(both, wide), high, low, near0, near1, near_over0, near_over1,
        halves, over_halves, *levels, eps, total, flops=2 * pair,
    )
    total = call(
        mate_kernel, shape(both, wide), high, low, mate0, mate1, mate_over0, mate_over1,
        halves, over_halves, *levels, eps, total, flops=2 * pair,
    )
    return call(
        far_kernel, shape(1, both, wide), high, low, far, far_over, *levels, eps, total,
        flops=3 * pair,
    )


def per_device(*arrays):
    blocks = lax.axis_size("blk")
    if lax.axis_size("rep") == 2 and TURNS == 2 and blocks % 2 == 0 and arrays[3].shape == (1,):
        return two_replicas(*arrays)
    return any_replicas(*arrays)


def solution(mesh):
    return jax.shard_map(
        per_device,
        mesh=mesh,
        in_specs=(P(None, "blk", None), P(None, "rep"), P(None, "rep"), P("blk"), P()),
        out_specs=P("blk", None, "rep"),
        check_vma=False,
    )
```

time: 73.2 us -> 67.1 us (0.917)
  waiting for transfers between devices: 40.1 us -> 34.7 us
  Pallas kernels: 18.5 us -> 14.1 us
  starting transfers between devices: 13.1 us -> 16.9 us
    ppermute x1 -> x2, waiting for transfers between devices: 14.9 us -> 10.9 us  [from_behind(): return lax.ppermute(x, axis, [(i, (i + by) % count) for i in range(count)])]
    ppermute x4 -> x7, waiting for transfers between devices: 11.2 us -> 7.81 us  [the longest x1 5.34 us: two_replicas(): near_over1 = lax.ppermute(near1, 'rep', swap)]
    ppermute x1 -> x2, starting transfers between devices: 0.62 us -> 2.87 us  [from_behind(): return lax.ppermute(x, axis, [(i, (i + by) % count) for i in range(count)])]
    pallas_call x4 -> x6, Pallas kernels: 12.2 us -> 9.95 us  [call(): pl.pallas_call(kernel, out_shape=out, in_specs=[vmem] * len(arrays), out_...]
    pallas_call x1, Pallas kernels: 6.32 us -> 4.18 us  [two_replicas(): pl.pallas_call(transform_kernel, in_specs=[anywhere, anywhere, pl.BlockSp...]
    ppermute x1, waiting for transfers between devices: 0.33 us -> 2.32 us  [two_replicas(): far_over = lax.ppermute(over, 'blk', past)]
    ppermute x4 -> x7, starting transfers between devices: 2 us -> 3.29 us  [the longest x1 1.5 us: two_replicas(): near_over0 = lax.ppermute(near0, 'rep', swap)]
  transfers between devices with their start and end apart: 10 -> 14, of which waited for: 6 -> 8; matrix products, arithmetic and copies ran while one was open for 0% -> 0% of each run, Pallas kernels for 10% -> 8%
where the time goes in v3:
time: 67.1 us; the launch traced here: 66.9 us
  waiting for transfers between devices  34.7 us (52%)
  starting transfers between devices  16.9 us (25%)
  Pallas kernels  14.1 us (21%)
  between operations  0.97 us (1%)
    ppermute x2, waiting for transfers between devices, from_behind(): return lax.ppermute(x, axis, [(i, (i + by) % count) for i in range(count)])  10.9 us
    pallas_call x6, Pallas kernels, call(): pl.pallas_call(kernel, out_shape=out, in_specs=[vmem] * len(arrays), out_...  9.95 us
    ppermute x1, waiting for transfers between devices, two_replicas(): there = lax.ppermute(quarter, 'rep', swap)  9.9 us
    all_to_all x1, starting transfers between devices, two_replicas(): got = lax.all_to_all(sent, 'blk', split_axis=0, concat_axis=0, tiled=True)  7.43 us
    ppermute x1, waiting for transfers between devices, two_replicas(): near_over1 = lax.ppermute(near1, 'rep', swap)  5.34 us
    pallas_call x1, Pallas kernels, two_replicas(): pl.pallas_call(transform_kernel, in_specs=[anywhere, anywhere, pl.BlockSp...  4.18 us
    ppermute x2, starting transfers between devices, from_behind(): return lax.ppermute(x, axis, [(i, (i + by) % count) for i in range(count)])  2.87 us
    ppermute x1, waiting for transfers between devices, two_replicas(): near_over0 = lax.ppermute(near0, 'rep', swap)  2.46 us
  transfers between devices with their start and end apart: 14, of which 8 were waited for; matrix products, arithmetic and copies ran while one was open for 0% of the time, Pallas kernels for 8%

profile of v3, /device:TPU:0, one launch (start us, length us, event | category | flops | bytes accessed | tf_op | source)
XLA Modules:
  0.0 66.9 jit_solution(12097534392122887895)
XLA Ops:
  0.8 4.2 %transform_kernel.1 = f32[16,72,128]{2,1,0:T(8,128)} custom-call(f32[16,64,512]{2,1,0:T(8,128)} %raw_hbm.1, f32[512,128]{1,0:T(8,128)} %coeffs_hbm.1, f32[1]{0:T(128)S(6)} %copy.10.eps_ref), custom_call_target="tpu_custom_call" | custom-call | flops 402653184 | bytes 2097152 | tf_op jit(solution)/shard_map/transform_kernel/pallas_call | solution.py:281
  5.0 7.4 %all-to-all-start = ((f32[16,72,128]{2,1,0:T(8,128)}), f32[16,72,128]{2,1,0:T(8,128)S(1)}, u32[]{:S(2)}, u32[]{:S(2)}) async-start(f32[16,72,128]{2,1,0:T(8,128)} %transform_kernel.1), calls=%async_computation | async-start | bytes 1179648 | tf_op jit(solution)/shard_map/all_to_all | solution.py:309
  12.5 0.0 copy-start.1
  12.6 1.6 %collective-permute-start = (f32[384,256]{1,0:T(8,128)S(1)}, f32[384,256]{1,0:T(8,128)S(1)}, u32[]{:S(2)}, u32[]{:S(2)}) collective-permute-start(f32[384,256]{1,0:T(8,128)S(1)} %pad_maximum_fusion), channel_id=1, source_target_pairs={{0,1},{1,0},{2,3},{3,2},{4,5},{5,4},{6,7},{7,6},{8,9},{9,8},{10,11... | collective-permute-start | bytes 1179656 | tf_op jit(solution)/shard_map/ppermute | solution.py:308
  14.1 9.9 %collective-permute-done.there_ref = f32[384,256]{1,0:T(8,128)S(1)} collective-permute-done((f32[384,256]{1,0:T(8,128)S(1)}, f32[384,256]{1,0:T(8,128)S(1)}, u32[]{:S(2)}, u32[]{:S(2)}) %collective-permute-start) | collective-permute-done | bytes 393248 | tf_op jit(solution)/shard_map/ppermute | solution.py:308
  24.0 0.0 collective-permute-start.1
  24.0 1.7 %collective-permute-done.1.mate_ref = f32[384,256]{1,0:T(8,128)S(1)} collective-permute-done((f32[384,256]{1,0:T(8,128)S(1)}, f32[384,256]{1,0:T(8,128)S(1)}, u32[]{:S(2)}, u32[]{:S(2)}) %collective-permute-start.1) | collective-permute-done | bytes 393248 | tf_op jit(solution)/shard_map/ppermute | solution.py:310
  25.8 2.0 %all-to-all-done.got_ref = f32[16,72,128]{2,1,0:T(8,128)S(1)} async-done(((f32[16,72,128]{2,1,0:T(8,128)}), f32[16,72,128]{2,1,0:T(8,128)S(1)}, u32[]{:S(2)}, u32[]{:S(2)}) %all-to-all-start) | async-done | bytes 589856 | tf_op jit(solution)/shard_map/all_to_all | solution.py:309
  27.8 2.4 %shard_map.55 = (f32[2,128,512]{2,1,0:T(8,128)}, f32[128,512]{1,0:T(8,128)S(1)}, f32[128,512]{1,0:T(8,128)S(1)}, f32[16,8,128]{2,1,0:T(8,128)S(1)}) custom-call(f32[16,72,128]{2,1,0:T(8,128)S(1)} %all-to-all-done.got_ref, f32[1024,512]{1,0:T(8,128)S(1)} %copy-done, f32[384,256]{1,0:T(8,128)S(1)} %collective-permute-done.there_ref, ...), custom_call_target="tpu_custom_call" | custom-call | flops 805306368 | bytes 4587520 | tf_op jit(solution)/shard_map/pallas_call | solution.py:254
  30.2 0.6 collective-permute-start.3
  30.8 1.5 %collective-permute-start.2 = (f32[2,128,512]{2,1,0:T(8,128)}, f32[2,128,512]{2,1,0:T(8,128)}, u32[]{:S(2)}, u32[]{:S(2)}) collective-permute-start(f32[2,128,512]{2,1,0:T(8,128)} %get-tuple-element.13.fit_ref), channel_id=1, source_target_pairs={{0,1},{1,0},{2,3},{3,2},{4,5},{5,4},{6,7},{7,6},{8,9},{9,8},{10,11... | collective-permute-start | bytes 1572872 | tf_op jit(solution)/shard_map/ppermute | solution.py:322
  32.3 2.3 %collective-permute-start.4 = (f32[128,512]{1,0:T(8,128)S(1)}, f32[128,512]{1,0:T(8,128)S(1)}, u32[]{:S(2)}, u32[]{:S(2)}) collective-permute-start(f32[128,512]{1,0:T(8,128)S(1)} %get-tuple-element.15), channel_id=1, source_target_pairs={{0,4},{2,6},{4,8},{6,10},{8,12},{10,14},{12,16},{14,18},{16,20},{1... | collective-permute-start | bytes 786440 | tf_op jit(solution)/shard_map/ppermute | solution.py:16
  34.6 7.5 %collective-permute-done.3.near0_ref = f32[128,512]{1,0:T(8,128)S(1)} collective-permute-done((f32[128,512]{1,0:T(8,128)S(1)}, f32[128,512]{1,0:T(8,128)S(1)}, u32[]{:S(2)}, u32[]{:S(2)}) %collective-permute-start.3) | collective-permute-done | bytes 262176 | tf_op jit(solution)/shard_map/ppermute | solution.py:16
  42.1 0.0 collective-permute-start.5
  42.1 1.5 %collective-permute-start.9 = (f32[128,512]{1,0:T(8,128)S(1)}, f32[128,512]{1,0:T(8,128)S(1)}, u32[]{:S(2)}, u32[]{:S(2)}) collective-permute-start(f32[128,512]{1,0:T(8,128)S(1)} %collective-permute-done.3.near0_ref), channel_id=1, source_target_pairs={{0,1},{1,0},{2,3},{3,2},{4,5},{5,4},{6,7},{7,6},{8,9},{9,8},{10,11... | collective-permute-start | bytes 786440 | tf_op jit(solution)/shard_map/ppermute | solution.py:324
  43.6 3.4 %collective-permute-done.4.near1_ref = f32[128,512]{1,0:T(8,128)S(1)} collective-permute-done((f32[128,512]{1,0:T(8,128)S(1)}, f32[128,512]{1,0:T(8,128)S(1)}, u32[]{:S(2)}, u32[]{:S(2)}) %collective-permute-start.4) | collective-permute-done | bytes 262176 | tf_op jit(solution)/shard_map/ppermute | solution.py:16
  47.0 1.5 %collective-permute-start.11 = (f32[128,512]{1,0:T(8,128)S(1)}, f32[128,512]{1,0:T(8,128)S(1)}, u32[]{:S(2)}, u32[]{:S(2)}) collective-permute-start(f32[128,512]{1,0:T(8,128)S(1)} %collective-permute-done.4.near1_ref), channel_id=1, source_target_pairs={{0,1},{1,0},{2,3},{3,2},{4,5},{5,4},{6,7},{7,6},{8,9},{9,8},{10,11... | collective-permute-start | bytes 786440 | tf_op jit(solution)/shard_map/ppermute | solution.py:327
  48.5 0.3 collective-permute-start.6
  48.7 0.2 collective-permute-start.8
  49.0 2.5 %collective-permute-done.9.near_over_ref.over0_ref = f32[128,512]{1,0:T(8,128)S(1)} collective-permute-done((f32[128,512]{1,0:T(8,128)S(1)}, f32[128,512]{1,0:T(8,128)S(1)}, u32[]{:S(2)}, u32[]{:S(2)}) %collective-permute-start.9) | collective-permute-done | bytes 262176 | tf_op jit(solution)/shard_map/ppermute | solution.py:324
  51.4 0.0 collective-permute-start.10
  51.4 5.3 %collective-permute-done.11.over1_ref = f32[128,512]{1,0:T(8,128)S(1)} collective-permute-done((f32[128,512]{1,0:T(8,128)S(1)}, f32[128,512]{1,0:T(8,128)S(1)}, u32[]{:S(2)}, u32[]{:S(2)}) %collective-permute-start.11) | collective-permute-done | bytes 262176 | tf_op jit(solution)/shard_map/ppermute | solution.py:327
  56.8 0.0 collective-permute-start.12
  56.8 0.1 copy.6.column_ref
  56.9 0.0 collective-permute-done.6.mate1_ref
  57.0 3.4 %shard_map.56 = (bf16[2,256,512]{2,1,0:T(8,128)(2,1)S(1)}, bf16[2,256,512]{2,1,0:T(8,128)(2,1)S(1)}, f32[256,256]{1,0:T(8,128)S(1)}, f32[256,512]{1,0:T(8,128)S(1)}) custom-call(f32[2,128,512]{2,1,0:T(8,128)} %get-tuple-element.13.fit_ref, f32[2,128,512]{2,1,0:T(8,128)} %collective-permute-done.2.over_ref, f32[128,512]{1,0:T(8,128)S(1)} %collective-permute-done.3.near0_ref, ...), custom_call_target="tpu_custom_call" | custom-call | flops 1006632960 | bytes 3999744 | tf_op jit(solution)/shard_map/pallas_call | solution.py:254
  60.4 0.4 shard_map.57.over_halves_ref
  60.8 0.8 %shard_map.58.sum_ref = f32[256,512]{1,0:T(8,128)S(1)} custom-call(bf16[2,256,512]{2,1,0:T(8,128)(2,1)S(1)} %get-tuple-element.17.high_ref, bf16[2,256,512]{2,1,0:T(8,128)(2,1)S(1)} %get-tuple-element.18.low_ref, f32[128,512]{1,0:T(8,128)S(1)} %collective-permute-done.3.near0_ref, f32[128,512]{1,0:T(8,128)S(1)} %collective-permute-done.4.near1_ref, ...), custom_call_target="tpu_custom_call" | custom-call | flops 402653184 | bytes 3737600 | tf_op jit(solution)/shard_map/pallas_call | solution.py:254
  61.6 0.8 %shard_map.59.sum_ref = f32[256,512]{1,0:T(8,128)S(1)} custom-call(bf16[2,256,512]{2,1,0:T(8,128)(2,1)S(1)} %get-tuple-element.17.high_ref, bf16[2,256,512]{2,1,0:T(8,128)(2,1)S(1)} %get-tuple-element.18.low_ref, f32[128,512]{1,0:T(8,128)S(1)} %collective-permute-done.5.mate0_ref, f32[128,512]{1,0:T(8,128)S(1)} %collective-permute-done.6.mate1_ref, ...), custom_call_target="tpu_custom_call" | custom-call | flops 402653184 | bytes 3737600 | tf_op jit(solution)/shard_map/pallas_call | solution.py:254
  62.4 0.0 collective-permute-done.7.far_ref
  62.4 2.3 %collective-permute-done.8.far_over_ref = f32[2,128,512]{2,1,0:T(8,128)S(1)} collective-permute-done((f32[2,128,512]{2,1,0:T(8,128)}, f32[2,128,512]{2,1,0:T(8,128)S(1)}, u32[]{:S(2)}, u32[]{:S(2)}) %collective-permute-start.8) | collective-permute-done | bytes 524320 | tf_op jit(solution)/shard_map/ppermute | solution.py:326
  64.7 2.2 %shard_map.60 = f32[1,256,512]{2,1,0:T(8,128)} custom-call(bf16[2,256,512]{2,1,0:T(8,128)(2,1)S(1)} %get-tuple-element.17.high_ref, bf16[2,256,512]{2,1,0:T(8,128)(2,1)S(1)} %get-tuple-element.18.low_ref, f32[2,128,512]{2,1,0:T(8,128)S(1)} %collective-permute-done.7.far_ref, f32[2,128,512]{2,1,0:T(8,128)S(1)} %collective-permute-done.8.far_over_ref, ...), custom_call_target="tpu_custom_call" | custom-call | flops 603979776 | bytes 3213312 | tf_op jit(solution)/shard_map/pallas_call | solution.py:254
  (13 shorter events, 0.1 us)
Async XLA Ops:
  0.0 12.5 %copy-start = (f32[1024,512]{1,0:T(8,128)S(1)}, f32[1024,512]{1,0:T(8,128)}, u32[]{:S(2)}) copy-start(f32[1024,512]{1,0:T(8,128)} %metric_ref.1) | copy-start | bytes 6291460
  5.0 22.8 %all-to-all-start = ((f32[16,72,128]{2,1,0:T(8,128)}), f32[16,72,128]{2,1,0:T(8,128)S(1)}, u32[]{:S(2)}, u32[]{:S(2)}) async-start(f32[16,72,128]{2,1,0:T(8,128)} %transform_kernel.1), calls=%async_computation | async-start | bytes 1179648 | tf_op jit(solution)/shard_map/all_to_all | solution.py:309
  12.5 36.5 %copy-start.1 = (f32[256]{0:T(256)S(1)}, f32[256]{0:T(256)}, u32[]{:S(2)}) copy-start(f32[256]{0:T(256)} %param.9) | copy-start | bytes 3076
  12.6 11.5 %collective-permute-start = (f32[384,256]{1,0:T(8,128)S(1)}, f32[384,256]{1,0:T(8,128)S(1)}, u32[]{:S(2)}, u32[]{:S(2)}) collective-permute-start(f32[384,256]{1,0:T(8,128)S(1)} %pad_maximum_fusion), channel_id=1, source_target_pairs={{0,1},{1,0},{2,3},{3,2},{4,5},{5,4},{6,7},{7,6},{8,9},{9,8},{10,11... | collective-permute-start | bytes 1179656 | tf_op jit(solution)/shard_map/ppermute | solution.py:308
  24.0 1.7 %collective-permute-start.1 = (f32[384,256]{1,0:T(8,128)S(1)}, f32[384,256]{1,0:T(8,128)S(1)}, u32[]{:S(2)}, u32[]{:S(2)}) collective-permute-start(f32[384,256]{1,0:T(8,128)S(1)} %collective-permute-done.there_ref), channel_id=1, source_target_pairs={{0,2},{2,0},{4,6},{6,4},{8,10},{10,8},{12,14},{14,12},{16,18},{18,... | collective-permute-start | bytes 1179656 | tf_op jit(solution)/shard_map/ppermute | solution.py:310
  30.2 11.9 %collective-permute-start.3 = (f32[128,512]{1,0:T(8,128)S(1)}, f32[128,512]{1,0:T(8,128)S(1)}, u32[]{:S(2)}, u32[]{:S(2)}) collective-permute-start(f32[128,512]{1,0:T(8,128)S(1)} %get-tuple-element.14), channel_id=1, source_target_pairs={{0,4},{2,6},{4,8},{6,10},{8,12},{10,14},{12,16},{14,18},{16,20},{1... | collective-permute-start | bytes 786440 | tf_op jit(solution)/shard_map/ppermute | solution.py:16
  30.8 17.9 %collective-permute-start.2 = (f32[2,128,512]{2,1,0:T(8,128)}, f32[2,128,512]{2,1,0:T(8,128)}, u32[]{:S(2)}, u32[]{:S(2)}) collective-permute-start(f32[2,128,512]{2,1,0:T(8,128)} %get-tuple-element.13.fit_ref), channel_id=1, source_target_pairs={{0,1},{1,0},{2,3},{3,2},{4,5},{5,4},{6,7},{7,6},{8,9},{9,8},{10,11... | collective-permute-start | bytes 1572872 | tf_op jit(solution)/shard_map/ppermute | solution.py:322
  32.3 14.6 %collective-permute-start.4 = (f32[128,512]{1,0:T(8,128)S(1)}, f32[128,512]{1,0:T(8,128)S(1)}, u32[]{:S(2)}, u32[]{:S(2)}) collective-permute-start(f32[128,512]{1,0:T(8,128)S(1)} %get-tuple-element.15), channel_id=1, source_target_pairs={{0,4},{2,6},{4,8},{6,10},{8,12},{10,14},{12,16},{14,18},{16,20},{1... | collective-permute-start | bytes 786440 | tf_op jit(solution)/shard_map/ppermute | solution.py:16
  42.1 6.4 %collective-permute-start.5 = (f32[128,512]{1,0:T(8,128)S(1)}, f32[128,512]{1,0:T(8,128)S(1)}, u32[]{:S(2)}, u32[]{:S(2)}) collective-permute-start(f32[128,512]{1,0:T(8,128)S(1)} %collective-permute-done.3.near0_ref), channel_id=1, source_target_pairs={{0,2},{2,0},{4,6},{6,4},{8,10},{10,8},{12,14},{14,12},{16,18},{18,... | collective-permute-start | bytes 786440 | tf_op jit(solution)/shard_map/ppermute | solution.py:328
  42.1 9.4 %collective-permute-start.9 = (f32[128,512]{1,0:T(8,128)S(1)}, f32[128,512]{1,0:T(8,128)S(1)}, u32[]{:S(2)}, u32[]{:S(2)}) collective-permute-start(f32[128,512]{1,0:T(8,128)S(1)} %collective-permute-done.3.near0_ref), channel_id=1, source_target_pairs={{0,1},{1,0},{2,3},{3,2},{4,5},{5,4},{6,7},{7,6},{8,9},{9,8},{10,11... | collective-permute-start | bytes 786440 | tf_op jit(solution)/shard_map/ppermute | solution.py:324
  47.0 9.8 %collective-permute-start.11 = (f32[128,512]{1,0:T(8,128)S(1)}, f32[128,512]{1,0:T(8,128)S(1)}, u32[]{:S(2)}, u32[]{:S(2)}) collective-permute-start(f32[128,512]{1,0:T(8,128)S(1)} %collective-permute-done.4.near1_ref), channel_id=1, source_target_pairs={{0,1},{1,0},{2,3},{3,2},{4,5},{5,4},{6,7},{7,6},{8,9},{9,8},{10,11... | collective-permute-start | bytes 786440 | tf_op jit(solution)/shard_map/ppermute | solution.py:327
  48.5 13.9 %collective-permute-start.7 = (f32[2,128,512]{2,1,0:T(8,128)}, f32[2,128,512]{2,1,0:T(8,128)S(1)}, u32[]{:S(2)}, u32[]{:S(2)}) collective-permute-start(f32[2,128,512]{2,1,0:T(8,128)} %get-tuple-element.13.fit_ref), channel_id=1, source_target_pairs={{0,2},{2,8},{4,6},{6,12},{8,10},{10,16},{12,14},{14,20},{16,18},{1... | collective-permute-start | bytes 1572872 | tf_op jit(solution)/shard_map/ppermute | solution.py:325
  48.5 8.5 %collective-permute-start.6 = (f32[128,512]{1,0:T(8,128)S(1)}, f32[128,512]{1,0:T(8,128)S(1)}, u32[]{:S(2)}, u32[]{:S(2)}) collective-permute-start(f32[128,512]{1,0:T(8,128)S(1)} %collective-permute-done.4.near1_ref), channel_id=1, source_target_pairs={{0,2},{2,0},{4,6},{6,4},{8,10},{10,8},{12,14},{14,12},{16,18},{18,... | collective-permute-start | bytes 786440 | tf_op jit(solution)/shard_map/ppermute | solution.py:329
  48.7 15.9 %collective-permute-start.8 = (f32[2,128,512]{2,1,0:T(8,128)}, f32[2,128,512]{2,1,0:T(8,128)S(1)}, u32[]{:S(2)}, u32[]{:S(2)}) collective-permute-start(f32[2,128,512]{2,1,0:T(8,128)} %collective-permute-done.2.over_ref), channel_id=1, source_target_pairs={{0,2},{2,8},{4,6},{6,12},{8,10},{10,16},{12,14},{14,20},{16,18},{1... | collective-permute-start | bytes 1572872 | tf_op jit(solution)/shard_map/ppermute | solution.py:326
  51.4 9.0 %collective-permute-start.10 = (f32[128,512]{1,0:T(8,128)S(1)}, f32[128,512]{1,0:T(8,128)S(1)}, u32[]{:S(2)}, u32[]{:S(2)}) collective-permute-start(f32[128,512]{1,0:T(8,128)S(1)} %collective-permute-done.9.near_over_ref.over0_ref), channel_id=1, source_target_pairs={{0,2},{2,0},{4,6},{6,4},{8,10},{10,8},{12,14},{14,12},{16,18},{18,... | collective-permute-start | bytes 786440 | tf_op jit(solution)/shard_map/ppermute | solution.py:340
  56.8 4.8 %collective-permute-start.12 = (f32[128,512]{1,0:T(8,128)S(1)}, f32[128,512]{1,0:T(8,128)S(1)}, u32[]{:S(2)}, u32[]{:S(2)}) collective-permute-start(f32[128,512]{1,0:T(8,128)S(1)} %collective-permute-done.11.over1_ref), channel_id=1, source_target_pairs={{0,2},{2,0},{4,6},{6,4},{8,10},{10,8},{12,14},{14,12},{16,18},{18,... | collective-permute-start | bytes 786440 | tf_op jit(solution)/shard_map/ppermute | solution.py:344

commit v4 on v3

--- a/solution.py
+++ b/solution.py
@@ -8,6 +8,7 @@
 from jax.sharding import PartitionSpec as P
 
 TURNS = 2
+OWN, NEAR, FAR, MATE = range(4)
 VMEM = 24 << 20
 
 
@@ -71,7 +72,7 @@
 
 
 def transform_kernel(
-    raw_hbm, coeffs_hbm, eps_ref, out_hbm, raw_ref, coeffs_ref, out_ref, coeffs_sem, in_sems, out_sems
+    raw_hbm, coeffs_hbm, out_hbm, raw_ref, coeffs_ref, out_ref, coeffs_sem, in_sems, out_sems
 ):
     steps = in_sems.shape[0]
     group = raw_ref.shape[0] // steps
@@ -89,7 +90,6 @@
     ]
     for copy in into:
         copy.start()
-    out_ref[:, depth:] = jnp.full((out_ref.shape[0], 8, rows), eps_ref[0], jnp.float32)
     first.wait()
     high, low = split(coeffs_ref[...])
     both = jnp.concatenate([high, low], 1)
@@ -101,22 +101,26 @@
         raw = split(raw_ref[at].reshape(group * depth, -1))
         wide = one(raw[0], both)
         done = wide[:, :rows] + (wide[:, rows:] + one(raw[1], high))
-        out_ref[at, :depth] = done.reshape(group, depth, rows)
+        out_ref[at] = done.reshape(group, depth, rows)
         out[step].start()
     for copy in out:
         copy.wait()
 
 
+def levels_kernel(own_eps, near_eps, far_eps, mate_eps, eps_ref):
+    for index, level in enumerate((own_eps, near_eps, far_eps, mate_eps)):
+        eps_ref[index] = jnp.broadcast_to(level[...], eps_ref.shape[1:])
+
+
 def fit_kernel(
-    got_ref, metric_ref, there_ref, mate_ref, out_ref, first_ref, second_ref, eps_ref,
+    got_ref, metric_ref, there_ref, mate_ref, out_ref, first_ref, second_ref,
     rows_high, rows_low, square_high, square_low,
 ):
     rep = lax.axis_index("rep")
     core = lax.axis_index("blk") % 2
-    depth = got_ref.shape[1] - 8
     wide = metric_ref.shape[1]
     half, step = wide // 2, wide // 4
-    rows = split(got_ref[:, :depth].reshape(-1, got_ref.shape[2]).T)
+    rows = split(got_ref[...].reshape(-1, got_ref.shape[2]).T)
     for part in range(2):
         at = slice(part * wide, (part + 1) * wide)
         rows_high[part], rows_low[part] = rows[0][:, at], rows[1][:, at]
@@ -138,7 +142,6 @@
     second_ref[...] = jnp.where(rep == 0, there, mine)
     out_ref[rep] = mine
     out_ref[1 - rep] = there
-    eps_ref[...] = got_ref[:, depth:]
 
 
 def beside(own, others):
@@ -183,8 +186,7 @@
         high_ref[half, size:], low_ref[half, size:] = split(over_ref[half])
     own = own_parts(high_ref, low_ref)
     whole = product(own[0], own[0], 1, 1) + product(own[1], own[1], 1, 1)
-    block = lax.axis_index("blk")
-    weights = amplitude(whole, levels_ref, column_ref, eps_ref, block, block)
+    weights = amplitude(whole, levels_ref, column_ref, eps_ref, OWN, OWN)
     total_ref[...] = gradient(weights, fit_ref[rep], over_ref[rep])
     halves_ref[...] = beside(own[0], [near0_ref[...], mate0_ref[...]]) + beside(
         own[1], [near1_ref[...], mate1_ref[...]]
@@ -196,11 +198,6 @@
     halves_ref[...] = beside(own, [near_over_ref[...], mate_over_ref[...]])
 
 
-def behind(by):
-    blocks = lax.axis_size("blk")
-    return lax.rem(lax.axis_index("blk") + blocks - by, blocks)
-
-
 def near_kernel(
     high_ref, low_ref, near0_ref, near1_ref, over0_ref, over1_ref, halves_ref, over_halves_ref,
     levels_ref, column_ref, eps_ref, sum_ref, total_ref,
@@ -208,8 +205,7 @@
     size = near0_ref.shape[0]
     late = over_halves_ref[:, :size] + beside((high_ref[1], low_ref[1]), [over1_ref[...]])
     whole = jnp.concatenate([halves_ref[:, :size], late], 1)
-    block = lax.axis_index("blk")
-    weights = amplitude(whole, levels_ref, column_ref, eps_ref, block, behind(2))
+    weights = amplitude(whole, levels_ref, column_ref, eps_ref, OWN, NEAR)
     total_ref[...] = sum_ref[...] + gradient(
         weights, half_here(near0_ref, near1_ref), half_here(over0_ref, over1_ref)
     )
@@ -222,9 +218,7 @@
     size = mate0_ref.shape[0]
     late = over_halves_ref[:, size:] + beside((high_ref[1], low_ref[1]), [over1_ref[...]])
     whole = jnp.concatenate([halves_ref[:, size:], late], 1)
-    block = lax.axis_index("blk")
-    other = jnp.where(block % 2 == 0, behind(1), behind(3))
-    weights = amplitude(whole, levels_ref, column_ref, eps_ref, block, other)
+    weights = amplitude(whole, levels_ref, column_ref, eps_ref, OWN, MATE)
     total_ref[...] = sum_ref[...] + gradient(
         weights, half_here(mate0_ref, mate1_ref), half_here(over0_ref, over1_ref)
     )
@@ -239,9 +233,7 @@
     whole = beside(own[0], [far_ref[0], far_over_ref[0]]) + beside(
         own[1], [far_ref[1], far_over_ref[1]]
     )
-    block = lax.axis_index("blk")
-    other = jnp.where(block % 2 == 0, behind(3), behind(1))
-    weights = amplitude(whole, levels_ref, column_ref, eps_ref, block, other)
+    weights = amplitude(whole, levels_ref, column_ref, eps_ref, OWN, FAR)
     total = sum_ref[...] + gradient(weights, far_ref[rep], far_over_ref[rep])
     out_ref[0, pl.ds(pl.multiple_of(rep * size, size), size)] = total[:size]
     out_ref[0, pl.ds(pl.multiple_of((1 - rep) * size, size), size)] = total[size:]
@@ -280,13 +272,13 @@
     anywhere = pl.BlockSpec(memory_space=pl.ANY)
     sent = pl.pallas_call(
         transform_kernel,
-        in_specs=[anywhere, anywhere, pl.BlockSpec(memory_space=pltpu.SMEM)],
+        in_specs=[anywhere, anywhere],
         out_specs=anywhere,
-        out_shape=shape(orbitals, depth + 8, rows),
+        out_shape=shape(orbitals, depth, rows),
         scratch_shapes=[
             pltpu.VMEM(raw_integrals.shape, jnp.float32),
             pltpu.VMEM(virtual_coeffs.shape, jnp.float32),
-            pltpu.VMEM((orbitals, depth + 8, rows), jnp.float32),
+            pltpu.VMEM((orbitals, depth, rows), jnp.float32),
             pltpu.SemaphoreType.DMA,
             pltpu.SemaphoreType.DMA((steps,)),
             pltpu.SemaphoreType.DMA((steps,)),
@@ -297,7 +289,7 @@
             transcendentals=0,
         ),
         name="transform_kernel",
-    )(raw_integrals, virtual_coeffs, occ_energies)
+    )(raw_integrals, virtual_coeffs)
     base, half, step = rep * wide, wide // 2, wide // 4
     quarter = jnp.concatenate(
         [
@@ -307,17 +299,22 @@
     )
     there = lax.ppermute(quarter, "rep", swap)
     got = lax.all_to_all(sent, "blk", split_axis=0, concat_axis=0, tiled=True)
+    past = [(i, (i + 1 + 2 * (i % 2)) % blocks) for i in range(blocks)]
+    near_eps = from_behind(occ_energies, "blk", 2)
+    far_eps = lax.ppermute(occ_energies, "blk", past)
+    mate_eps = lax.ppermute(
+        occ_energies, "blk", [(i, ((i + 2) % blocks) ^ 1) for i in range(blocks)]
+    )
     there_mate = lax.ppermute(there, "blk", mate)
     piece = shape(rows, wide)
-    fit, first, second, eps = call(
+    fit, first, second = call(
         fit_kernel,
-        (shape(2, rows, wide), piece, piece, shape(blocks, 8, rows)),
+        (shape(2, rows, wide), piece, piece),
         got, metric_root, there, there_mate,
         flops=6 * aux * aux * rows,
         scratch=[pltpu.VMEM((2, rows, wide), jnp.bfloat16)] * 2
         + [pltpu.VMEM((wide, wide), jnp.bfloat16)] * 2,
     )
-    past = [(i, (i + 1 + 2 * (i % 2)) % blocks) for i in range(blocks)]
     near0 = from_behind(first, "blk", 2)
     over = lax.ppermute(fit, "rep", swap)
     near1 = from_behind(second, "blk", 2)
@@ -327,6 +324,10 @@
     near_over1 = lax.ppermute(near1, "rep", swap)
     mate0 = lax.ppermute(near0, "blk", mate)
     mate1 = lax.ppermute(near1, "blk", mate)
+    eps = call(
+        levels_kernel, shape(4, 8, rows),
+        *(a.reshape(1, 1) for a in (occ_energies, near_eps, far_eps, mate_eps)), flops=0,
+    )
     levels = jnp.where(rep == 0, virt_energies, jnp.roll(virt_energies, rows))
     levels = (levels[None, :], levels[:, None])
     both = 2 * rows

time: 67.1 us -> 82.3 us (1.23)
  waiting for transfers between devices: 34.7 us -> 47.6 us
  Pallas kernels: 14.1 us -> 16.2 us
    ppermute x0 -> x2, waiting for transfers between devices: none -> 10.7 us  [the longest x1 5.77 us: two_replicas(): lax.ppermute(occ_energies, 'blk', [(i, (i + 2) % blocks ^ 1) for i in ran...]
    ppermute x2 -> x3, waiting for transfers between devices: 10.9 us -> 17.4 us  [from_behind(): return lax.ppermute(x, axis, [(i, (i + by) % count) for i in range(count)])]
    ppermute x1, waiting for transfers between devices: 5.34 us -> 0.01 us  [two_replicas(): near_over1 = lax.ppermute(near1, 'rep', swap)]
    ppermute x1, waiting for transfers between devices: 2.32 us -> 5.62 us  [two_replicas(): far_over = lax.ppermute(over, 'blk', past)]
    ppermute x1, waiting for transfers between devices: 2.46 us -> 0.01 us  [two_replicas(): near_over0 = lax.ppermute(near0, 'rep', swap)]
    pallas_call x6 -> x7, Pallas kernels: 9.95 us -> 11.9 us  [call(): pl.pallas_call(kernel, out_shape=out, in_specs=[vmem] * len(arrays), out_...]
    ppermute x1, waiting for transfers between devices: 0.01 us -> 1.3 us  [two_replicas(): far = lax.ppermute(fit, 'blk', past)]
    all_to_all x1, waiting for transfers between devices: 2.04 us -> 0.94 us  [two_replicas(): got = lax.all_to_all(sent, 'blk', split_axis=0, concat_axis=0, tiled=True)]
  transfers between devices with their start and end apart: 14 -> 17, of which waited for: 8 -> 10; matrix products, arithmetic and copies ran while one was open for 0% -> 0% of each run, Pallas kernels for 8% -> 9%
where the time goes in v4:
time: 82.3 us; the launch traced here: 82 us
  waiting for transfers between devices  47.6 us (58%)
  starting transfers between devices  17.2 us (21%)
  Pallas kernels  16.2 us (20%)
    ppermute x3, waiting for transfers between devices, from_behind(): return lax.ppermute(x, axis, [(i, (i + by) % count) for i in range(count)])  17.4 us
    pallas_call x7, Pallas kernels, call(): pl.pallas_call(kernel, out_shape=out, in_specs=[vmem] * len(arrays), out_...  11.9 us
    ppermute x1, waiting for transfers between devices, two_replicas(): there = lax.ppermute(quarter, 'rep', swap)  9.9 us
    all_to_all x1, starting transfers between devices, two_replicas(): got = lax.all_to_all(sent, 'blk', split_axis=0, concat_axis=0, tiled=True)  7.43 us
    ppermute x1, waiting for transfers between devices, two_replicas(): lax.ppermute(occ_energies, 'blk', [(i, (i + 2) % blocks ^ 1) for i in ran...  5.77 us
    ppermute x1, waiting for transfers between devices, two_replicas(): far_over = lax.ppermute(over, 'blk', past)  5.62 us
    ppermute x1, waiting for transfers between devices, two_replicas(): far_eps = lax.ppermute(occ_energies, 'blk', past)  4.88 us
    pallas_call x1, Pallas kernels, two_replicas(): pl.pallas_call(transform_kernel, in_specs=[anywhere, anywhere], out_specs...  4.32 us
  transfers between devices with their start and end apart: 17, of which 10 were waited for; matrix products, arithmetic and copies ran while one was open for 0% of the time, Pallas kernels for 9%

profile of v4, /device:TPU:0, one launch (start us, length us, event | category | flops | bytes accessed | tf_op | source)
XLA Modules:
  0.0 82.0 jit_solution(11473534481395636760)
XLA Ops:
  0.0 4.3 %transform_kernel.1 = f32[16,64,128]{2,1,0:T(8,128)} custom-call(f32[16,64,512]{2,1,0:T(8,128)} %raw_hbm.1, f32[512,128]{1,0:T(8,128)} %coeffs_hbm.1), custom_call_target="tpu_custom_call" | custom-call | flops 402653184 | bytes 2097152 | tf_op jit(solution)/shard_map/transform_kernel/pallas_call | solution.py:273
  4.3 7.4 %all-to-all-start = ((f32[16,64,128]{2,1,0:T(8,128)}), f32[16,64,128]{2,1,0:T(8,128)S(1)}, u32[]{:S(2)}, u32[]{:S(2)}) async-start(f32[16,64,128]{2,1,0:T(8,128)} %transform_kernel.1), calls=%async_computation | async-start | bytes 1048576 | tf_op jit(solution)/shard_map/all_to_all | solution.py:301
  11.9 0.0 copy-start.1
  11.9 1.6 %collective-permute-start = (f32[384,256]{1,0:T(8,128)S(1)}, f32[384,256]{1,0:T(8,128)S(1)}, u32[]{:S(2)}, u32[]{:S(2)}) collective-permute-start(f32[384,256]{1,0:T(8,128)S(1)} %pad_maximum_fusion), channel_id=1, source_target_pairs={{0,1},{1,0},{2,3},{3,2},{4,5},{5,4},{6,7},{7,6},{8,9},{9,8},{10,11... | collective-permute-start | bytes 1179656 | tf_op jit(solution)/shard_map/ppermute | solution.py:300
  13.5 9.9 %collective-permute-done.there_ref = f32[384,256]{1,0:T(8,128)S(1)} collective-permute-done((f32[384,256]{1,0:T(8,128)S(1)}, f32[384,256]{1,0:T(8,128)S(1)}, u32[]{:S(2)}, u32[]{:S(2)}) %collective-permute-start) | collective-permute-done | bytes 393248 | tf_op jit(solution)/shard_map/ppermute | solution.py:300
  23.4 1.7 %collective-permute-done.1.mate_ref = f32[384,256]{1,0:T(8,128)S(1)} collective-permute-done((f32[384,256]{1,0:T(8,128)S(1)}, f32[384,256]{1,0:T(8,128)S(1)}, u32[]{:S(2)}, u32[]{:S(2)}) %collective-permute-start.1) | collective-permute-done | bytes 393248 | tf_op jit(solution)/shard_map/ppermute | solution.py:308
  25.1 0.9 %all-to-all-done.got_ref = f32[16,64,128]{2,1,0:T(8,128)S(1)} async-done(((f32[16,64,128]{2,1,0:T(8,128)}), f32[16,64,128]{2,1,0:T(8,128)S(1)}, u32[]{:S(2)}, u32[]{:S(2)}) %all-to-all-start) | async-done | bytes 524320 | tf_op jit(solution)/shard_map/all_to_all | solution.py:301
  26.0 2.4 %shard_map.55 = (f32[2,128,512]{2,1,0:T(8,128)}, f32[128,512]{1,0:T(8,128)S(1)}, f32[128,512]{1,0:T(8,128)S(1)}) custom-call(f32[16,64,128]{2,1,0:T(8,128)S(1)} %all-to-all-done.got_ref, f32[1024,512]{1,0:T(8,128)S(1)} %copy-done, f32[384,256]{1,0:T(8,128)S(1)} %collective-permute-done.there_ref, f32[384,256]{1,0:T(8,128)S(1)} %collective-permute-done.1.mate_ref), custom_call_target="tpu_custom_call" | custom-call | flops 805306368 | bytes 4456448 | tf_op jit(solution)/shard_map/pallas_call | solution.py:246
  28.4 0.7 collective-permute-start.3
  29.1 1.5 %collective-permute-start.2 = (f32[2,128,512]{2,1,0:T(8,128)}, f32[2,128,512]{2,1,0:T(8,128)}, u32[]{:S(2)}, u32[]{:S(2)}) collective-permute-start(f32[2,128,512]{2,1,0:T(8,128)} %get-tuple-element.12.fit_ref), channel_id=1, source_target_pairs={{0,1},{1,0},{2,3},{3,2},{4,5},{5,4},{6,7},{7,6},{8,9},{9,8},{10,11... | collective-permute-start | bytes 1572872 | tf_op jit(solution)/shard_map/ppermute | solution.py:319
  30.6 1.9 %collective-permute-start.4 = (f32[128,512]{1,0:T(8,128)S(1)}, f32[128,512]{1,0:T(8,128)S(1)}, u32[]{:S(2)}, u32[]{:S(2)}) collective-permute-start(f32[128,512]{1,0:T(8,128)S(1)} %get-tuple-element.14), channel_id=1, source_target_pairs={{0,4},{2,6},{4,8},{6,10},{8,12},{10,14},{12,16},{14,18},{16,20},{1... | collective-permute-start | bytes 786440 | tf_op jit(solution)/shard_map/ppermute | solution.py:17
  32.5 7.8 %collective-permute-done.3.near0_ref = f32[128,512]{1,0:T(8,128)S(1)} collective-permute-done((f32[128,512]{1,0:T(8,128)S(1)}, f32[128,512]{1,0:T(8,128)S(1)}, u32[]{:S(2)}, u32[]{:S(2)}) %collective-permute-start.3) | collective-permute-done | bytes 262176 | tf_op jit(solution)/shard_map/ppermute | solution.py:17
  40.3 1.5 %collective-permute-start.12 = (f32[128,512]{1,0:T(8,128)S(1)}, f32[128,512]{1,0:T(8,128)S(1)}, u32[]{:S(2)}, u32[]{:S(2)}) collective-permute-start(f32[128,512]{1,0:T(8,128)S(1)} %collective-permute-done.3.near0_ref), channel_id=1, source_target_pairs={{0,1},{1,0},{2,3},{3,2},{4,5},{5,4},{6,7},{7,6},{8,9},{9,8},{10,11... | collective-permute-start | bytes 786440 | tf_op jit(solution)/shard_map/ppermute | solution.py:321
  41.8 3.3 %collective-permute-done.4.near1_ref = f32[128,512]{1,0:T(8,128)S(1)} collective-permute-done((f32[128,512]{1,0:T(8,128)S(1)}, f32[128,512]{1,0:T(8,128)S(1)}, u32[]{:S(2)}, u32[]{:S(2)}) %collective-permute-start.4) | collective-permute-done | bytes 262176 | tf_op jit(solution)/shard_map/ppermute | solution.py:17
  45.1 1.5 %collective-permute-start.14 = (f32[128,512]{1,0:T(8,128)S(1)}, f32[128,512]{1,0:T(8,128)S(1)}, u32[]{:S(2)}, u32[]{:S(2)}) collective-permute-start(f32[128,512]{1,0:T(8,128)S(1)} %collective-permute-done.4.near1_ref), channel_id=1, source_target_pairs={{0,1},{1,0},{2,3},{3,2},{4,5},{5,4},{6,7},{7,6},{8,9},{9,8},{10,11... | collective-permute-start | bytes 786440 | tf_op jit(solution)/shard_map/ppermute | solution.py:324
  46.6 6.3 %collective-permute-done.7 = f32[1]{0:T(128)} collective-permute-done((f32[1]{0:T(128)}, f32[1]{0:T(128)}, u32[]{:S(2)}, u32[]{:S(2)}) %collective-permute-start.7) | collective-permute-done | bytes 36 | tf_op jit(solution)/shard_map/ppermute | solution.py:17
  53.0 4.9 %collective-permute-done.8 = f32[1]{0:T(128)} collective-permute-done((f32[1]{0:T(128)}, f32[1]{0:T(128)}, u32[]{:S(2)}, u32[]{:S(2)}) %collective-permute-start.8) | collective-permute-done | bytes 36 | tf_op jit(solution)/shard_map/ppermute | solution.py:304
  57.8 0.0 collective-permute-start.9
  57.8 5.8 %collective-permute-done.9 = f32[1]{0:T(128)} collective-permute-done((f32[1]{0:T(128)}, f32[1]{0:T(128)}, u32[]{:S(2)}, u32[]{:S(2)}) %collective-permute-start.9) | collective-permute-done | bytes 36 | tf_op jit(solution)/shard_map/ppermute | solution.py:305
  63.6 0.0 collective-permute-start.10
  63.6 0.5 collective-permute-start.11
  64.2 0.1 collective-permute-start.13
  64.2 0.5 collective-permute-start.15
  65.4 0.1 copy.6.column_ref
  65.5 2.0 %shard_map.56.eps_ref = f32[4,8,128]{2,1,0:T(8,128)S(1)} custom-call(f32[1,1]{1,0:T(1,128)} %bitcast.6.own_eps, f32[1,1]{1,0:T(1,128)} %bitcast.3.near_eps, f32[1,1]{1,0:T(1,128)} %bitcast.4.far_eps, f32[1,1]{1,0:T(1,128)} %bitcast.5.mate_eps), custom_call_target="tpu_custom_call" | custom-call | bytes 16400 | tf_op jit(solution)/shard_map/pallas_call | solution.py:246
  67.5 3.4 %shard_map.57 = (bf16[2,256,512]{2,1,0:T(8,128)(2,1)S(1)}, bf16[2,256,512]{2,1,0:T(8,128)(2,1)S(1)}, f32[256,256]{1,0:T(8,128)S(1)}, f32[256,512]{1,0:T(8,128)S(1)}) custom-call(f32[2,128,512]{2,1,0:T(8,128)} %get-tuple-element.12.fit_ref, f32[2,128,512]{2,1,0:T(8,128)} %collective-permute-done.2.over_ref, f32[128,512]{1,0:T(8,128)S(1)} %collective-permute-done.3.near0_ref, ...), custom_call_target="tpu_custom_call" | custom-call | flops 1006632960 | bytes 3950592 | tf_op jit(solution)/shard_map/pallas_call | solution.py:246
  71.0 0.4 shard_map.58.over_halves_ref
  71.4 0.8 shard_map.59.sum_ref
  72.2 0.8 shard_map.60.sum_ref
  72.9 1.3 %collective-permute-done.10.far_ref = f32[2,128,512]{2,1,0:T(8,128)S(1)} collective-permute-done((f32[2,128,512]{2,1,0:T(8,128)}, f32[2,128,512]{2,1,0:T(8,128)S(1)}, u32[]{:S(2)}, u32[]{:S(2)}) %collective-permute-start.10) | collective-permute-done | bytes 524320 | tf_op jit(solution)/shard_map/ppermute | solution.py:322
  74.2 5.6 %collective-permute-done.11.far_over_ref = f32[2,128,512]{2,1,0:T(8,128)S(1)} collective-permute-done((f32[2,128,512]{2,1,0:T(8,128)}, f32[2,128,512]{2,1,0:T(8,128)S(1)}, u32[]{:S(2)}, u32[]{:S(2)}) %collective-permute-start.11) | collective-permute-done | bytes 524320 | tf_op jit(solution)/shard_map/ppermute | solution.py:323
  79.8 2.2 %shard_map.61 = f32[1,256,512]{2,1,0:T(8,128)} custom-call(bf16[2,256,512]{2,1,0:T(8,128)(2,1)S(1)} %get-tuple-element.15.high_ref, bf16[2,256,512]{2,1,0:T(8,128)(2,1)S(1)} %get-tuple-element.16.low_ref, f32[2,128,512]{2,1,0:T(8,128)S(1)} %collective-permute-done.10.far_ref, f32[2,128,512]{2,1,0:T(8,128)S(1)} %collective-permute-done.11.far_over_ref, ...), custom_call_target="tpu_custom_call" | custom-call | flops 603979776 | bytes 3164160 | tf_op jit(solution)/shard_map/pallas_call | solution.py:246
  (20 shorter events, 0.1 us)
Async XLA Ops:
  0.0 11.8 %copy-start = (f32[1024,512]{1,0:T(8,128)S(1)}, f32[1024,512]{1,0:T(8,128)}, u32[]{:S(2)}) copy-start(f32[1024,512]{1,0:T(8,128)} %metric_ref.1) | copy-start | bytes 6291460
  4.3 21.7 %all-to-all-start = ((f32[16,64,128]{2,1,0:T(8,128)}), f32[16,64,128]{2,1,0:T(8,128)S(1)}, u32[]{:S(2)}, u32[]{:S(2)}) async-start(f32[16,64,128]{2,1,0:T(8,128)} %transform_kernel.1), calls=%async_computation | async-start | bytes 1048576 | tf_op jit(solution)/shard_map/all_to_all | solution.py:301
  11.9 52.3 %copy-start.1 = (f32[256]{0:T(256)S(1)}, f32[256]{0:T(256)}, u32[]{:S(2)}) copy-start(f32[256]{0:T(256)} %param.9) | copy-start | bytes 3076
  11.9 11.5 %collective-permute-start = (f32[384,256]{1,0:T(8,128)S(1)}, f32[384,256]{1,0:T(8,128)S(1)}, u32[]{:S(2)}, u32[]{:S(2)}) collective-permute-start(f32[384,256]{1,0:T(8,128)S(1)} %pad_maximum_fusion), channel_id=1, source_target_pairs={{0,1},{1,0},{2,3},{3,2},{4,5},{5,4},{6,7},{7,6},{8,9},{9,8},{10,11... | collective-permute-start | bytes 1179656 | tf_op jit(solution)/shard_map/ppermute | solution.py:300
  23.4 1.7 %collective-permute-start.1 = (f32[384,256]{1,0:T(8,128)S(1)}, f32[384,256]{1,0:T(8,128)S(1)}, u32[]{:S(2)}, u32[]{:S(2)}) collective-permute-start(f32[384,256]{1,0:T(8,128)S(1)} %collective-permute-done.there_ref), channel_id=1, source_target_pairs={{0,2},{2,0},{4,6},{6,4},{8,10},{10,8},{12,14},{14,12},{16,18},{18,... | collective-permute-start | bytes 1179656 | tf_op jit(solution)/shard_map/ppermute | solution.py:308
  28.4 11.9 %collective-permute-start.3 = (f32[128,512]{1,0:T(8,128)S(1)}, f32[128,512]{1,0:T(8,128)S(1)}, u32[]{:S(2)}, u32[]{:S(2)}) collective-permute-start(f32[128,512]{1,0:T(8,128)S(1)} %get-tuple-element.13), channel_id=1, source_target_pairs={{0,4},{2,6},{4,8},{6,10},{8,12},{10,14},{12,16},{14,18},{16,20},{1... | collective-permute-start | bytes 786440 | tf_op jit(solution)/shard_map/ppermute | solution.py:17
  29.1 34.5 %collective-permute-start.2 = (f32[2,128,512]{2,1,0:T(8,128)}, f32[2,128,512]{2,1,0:T(8,128)}, u32[]{:S(2)}, u32[]{:S(2)}) collective-permute-start(f32[2,128,512]{2,1,0:T(8,128)} %get-tuple-element.12.fit_ref), channel_id=1, source_target_pairs={{0,1},{1,0},{2,3},{3,2},{4,5},{5,4},{6,7},{7,6},{8,9},{9,8},{10,11... | collective-permute-start | bytes 1572872 | tf_op jit(solution)/shard_map/ppermute | solution.py:319
  30.6 14.5 %collective-permute-start.4 = (f32[128,512]{1,0:T(8,128)S(1)}, f32[128,512]{1,0:T(8,128)S(1)}, u32[]{:S(2)}, u32[]{:S(2)}) collective-permute-start(f32[128,512]{1,0:T(8,128)S(1)} %get-tuple-element.14), channel_id=1, source_target_pairs={{0,4},{2,6},{4,8},{6,10},{8,12},{10,14},{12,16},{14,18},{16,20},{1... | collective-permute-start | bytes 786440 | tf_op jit(solution)/shard_map/ppermute | solution.py:17
  40.3 23.3 %collective-permute-start.5 = (f32[128,512]{1,0:T(8,128)S(1)}, f32[128,512]{1,0:T(8,128)S(1)}, u32[]{:S(2)}, u32[]{:S(2)}) collective-permute-start(f32[128,512]{1,0:T(8,128)S(1)} %collective-permute-done.3.near0_ref), channel_id=1, source_target_pairs={{0,2},{2,0},{4,6},{6,4},{8,10},{10,8},{12,14},{14,12},{16,18},{18,... | collective-permute-start | bytes 786440 | tf_op jit(solution)/shard_map/ppermute | solution.py:325
  40.3 23.8 %collective-permute-start.12 = (f32[128,512]{1,0:T(8,128)S(1)}, f32[128,512]{1,0:T(8,128)S(1)}, u32[]{:S(2)}, u32[]{:S(2)}) collective-permute-start(f32[128,512]{1,0:T(8,128)S(1)} %collective-permute-done.3.near0_ref), channel_id=1, source_target_pairs={{0,1},{1,0},{2,3},{3,2},{4,5},{5,4},{6,7},{7,6},{8,9},{9,8},{10,11... | collective-permute-start | bytes 786440 | tf_op jit(solution)/shard_map/ppermute | solution.py:321
  45.1 19.1 %collective-permute-start.14 = (f32[128,512]{1,0:T(8,128)S(1)}, f32[128,512]{1,0:T(8,128)S(1)}, u32[]{:S(2)}, u32[]{:S(2)}) collective-permute-start(f32[128,512]{1,0:T(8,128)S(1)} %collective-permute-done.4.near1_ref), channel_id=1, source_target_pairs={{0,1},{1,0},{2,3},{3,2},{4,5},{5,4},{6,7},{7,6},{8,9},{9,8},{10,11... | collective-permute-start | bytes 786440 | tf_op jit(solution)/shard_map/ppermute | solution.py:324
  46.6 6.4 %collective-permute-start.7 = (f32[1]{0:T(128)}, f32[1]{0:T(128)}, u32[]{:S(2)}, u32[]{:S(2)}) collective-permute-start(f32[1]{0:T(128)} %param.8), channel_id=1, source_target_pairs={{0,4},{2,6},{4,8},{6,10},{8,12},{10,14},{12,16},{14,18},{16,20},{1... | collective-permute-start | bytes 20 | tf_op jit(solution)/shard_map/ppermute | solution.py:17
  53.0 4.9 %collective-permute-start.8 = (f32[1]{0:T(128)}, f32[1]{0:T(128)}, u32[]{:S(2)}, u32[]{:S(2)}) collective-permute-start(f32[1]{0:T(128)} %param.8), channel_id=1, source_target_pairs={{0,2},{2,8},{4,6},{6,12},{8,10},{10,16},{12,14},{14,20},{16,18},{1... | collective-permute-start | bytes 20 | tf_op jit(solution)/shard_map/ppermute | solution.py:304
  57.8 5.8 %collective-permute-start.9 = (f32[1]{0:T(128)}, f32[1]{0:T(128)}, u32[]{:S(2)}, u32[]{:S(2)}) collective-permute-start(f32[1]{0:T(128)} %param.8), channel_id=1, source_target_pairs={{0,6},{2,4},{4,10},{6,8},{8,14},{10,12},{12,18},{14,16},{16,22},{1... | collective-permute-start | bytes 20 | tf_op jit(solution)/shard_map/ppermute | solution.py:305
  63.6 10.6 %collective-permute-start.10 = (f32[2,128,512]{2,1,0:T(8,128)}, f32[2,128,512]{2,1,0:T(8,128)S(1)}, u32[]{:S(2)}, u32[]{:S(2)}) collective-permute-start(f32[2,128,512]{2,1,0:T(8,128)} %get-tuple-element.12.fit_ref), channel_id=1, source_target_pairs={{0,2},{2,8},{4,6},{6,12},{8,10},{10,16},{12,14},{14,20},{16,18},{1... | collective-permute-start | bytes 1572872 | tf_op jit(solution)/shard_map/ppermute | solution.py:322
  63.6 3.9 %collective-permute-start.6 = (f32[128,512]{1,0:T(8,128)S(1)}, f32[128,512]{1,0:T(8,128)S(1)}, u32[]{:S(2)}, u32[]{:S(2)}) collective-permute-start(f32[128,512]{1,0:T(8,128)S(1)} %collective-permute-done.4.near1_ref), channel_id=1, source_target_pairs={{0,2},{2,0},{4,6},{6,4},{8,10},{10,8},{12,14},{14,12},{16,18},{18,... | collective-permute-start | bytes 786440 | tf_op jit(solution)/shard_map/ppermute | solution.py:326
  63.6 16.2 %collective-permute-start.11 = (f32[2,128,512]{2,1,0:T(8,128)}, f32[2,128,512]{2,1,0:T(8,128)S(1)}, u32[]{:S(2)}, u32[]{:S(2)}) collective-permute-start(f32[2,128,512]{2,1,0:T(8,128)} %collective-permute-done.2.over_ref), channel_id=1, source_target_pairs={{0,2},{2,8},{4,6},{6,12},{8,10},{10,16},{12,14},{14,20},{16,18},{1... | collective-permute-start | bytes 1572872 | tf_op jit(solution)/shard_map/ppermute | solution.py:323
  64.2 6.8 %collective-permute-start.13 = (f32[128,512]{1,0:T(8,128)S(1)}, f32[128,512]{1,0:T(8,128)S(1)}, u32[]{:S(2)}, u32[]{:S(2)}) collective-permute-start(f32[128,512]{1,0:T(8,128)S(1)} %collective-permute-done.12.near_over_ref.over0_ref), channel_id=1, source_target_pairs={{0,2},{2,0},{4,6},{6,4},{8,10},{10,8},{12,14},{14,12},{16,18},{18,... | collective-permute-start | bytes 786440 | tf_op jit(solution)/shard_map/ppermute | solution.py:341
  64.2 7.9 %collective-permute-start.15 = (f32[128,512]{1,0:T(8,128)S(1)}, f32[128,512]{1,0:T(8,128)S(1)}, u32[]{:S(2)}, u32[]{:S(2)}) collective-permute-start(f32[128,512]{1,0:T(8,128)S(1)} %collective-permute-done.14.over1_ref), channel_id=1, source_target_pairs={{0,2},{2,0},{4,6},{6,4},{8,10},{10,8},{12,14},{14,12},{16,18},{18,... | collective-permute-start | bytes 786440 | tf_op jit(solution)/shard_map/ppermute | solution.py:345
